TPU v7x, 32 devices: a whole 2x2x4 slice. The times are simulated.
32 devices in a mesh: tile: 8 (over z, x), depth: 4 (over y, core).
Axes of the slice: x: 2, y: 2, z: 4, core: 2. Of those that a mesh axis runs over, the one named last changes fastest.
Arguments:
- density: float32 [64, 128, 128], P('depth', 'tile'), may hold values from 0.5 to 2
- momentum: float32 [3, 64, 128, 128], P(None, 'depth', 'tile'), may hold values from -4 to 4
- magnetic: float32 [3, 64, 128, 128], P(None, 'depth', 'tile'), may hold values from -4 to 4
- energy: float32 [64, 128, 128], P('depth', 'tile'), may hold values from 2 to 4
- shifts: int32 [24], replicated, may hold values from 0 to 55, as said below
- levels: int32 [24], replicated, may hold values from 0 to 63, as said below
Outputs:
- new_state: float32 [8, 64, 128, 128], P(None, 'depth', 'tile')
- intensity: float32 [48, 128, 128], P(None, 'tile', 'depth')
Inputs may be any that keep to these rules, and one draw needn't show every extreme that they name: shifts[k] = (1732 (levels[k] - levels[0]) + 1000) // 2000, the nearest whole column to tan(60 degrees) times the depth gap at half a column per level; the last is exactly 55. 24 distinct levels in ascending order, the first 0 and the last 63; each depth slab of 16 consecutive levels holds at most 8 of them, and some slab exactly 8.
All inputs are finite; a program needn't handle non-finite values.
Results may differ from a plain program's by a relative error of at most 0.000054.
Values sent between devices are 32-bit elements; how exact they have to be, the bound alone decides.
A program may use at most 64 MiB of HBM per device.

v0:
```python
import jax
import jax.numpy as jnp
from jax import lax
from jax.sharding import PartitionSpec as P

W = 48
MOST = 8


GAMMA = 5.0 / 3.0
SECTION = 0.02
GRAVITY = 0.5
SIN_VIEW = 0.8660254037844386
COS_VIEW = 0.5
STRENGTH = 4.0
SPACING = 0.25


def shifted(block, axis, distance):
    devices = range(lax.axis_size(axis))
    route = [((i - distance) % len(devices), i) for i in devices]
    return lax.ppermute(block, axis, route)


def padded_2(cells, sides, width, closed):
    for axis, dim in sides:
        count = lax.axis_size(axis)
        ends = count if closed else count - 1
        head = lax.slice_in_dim(cells, 0, width, axis=dim)
        tail = lax.slice_in_dim(cells, cells.shape[dim] - width, cells.shape[dim], axis=dim)
        cells = jnp.concatenate(
            [
                lax.ppermute(tail, axis, [(i, (i + 1) % count) for i in range(ends)]),
                cells,
                lax.ppermute(head, axis, [((i + 1) % count, i) for i in range(ends)]),
            ],
            axis=dim,
        )
    return cells


def derive(padded, axis, count):

    def layer(offset):
        return lax.slice_in_dim(padded, offset, offset + count, axis=axis)

    return (
        45.0 * (layer(4) - layer(2)) - 9.0 * (layer(5) - layer(1)) + (layer(6) - layer(0))
    ) / 60.0


def flux(state, comp):
    rho = state[0]
    moment = state[1:4]
    field = state[4:7]
    energy = state[7]
    velocity = moment / rho
    field_sq = jnp.sum(field * field, axis=0)
    pressure = (GAMMA - 1.0) * (energy - 0.5 * jnp.sum(moment * velocity, axis=0) - 0.5 * field_sq)
    total = pressure + 0.5 * field_sq
    along = velocity[comp]
    normal = field[comp]
    flux_mom = (moment * along - field * normal).at[comp].add(total)
    flux_mag = along * field - normal * velocity
    flux_energy = (energy + total) * along - normal * jnp.sum(velocity * field, axis=0)
    return jnp.concatenate([moment[comp][None], flux_mom, flux_mag, flux_energy[None]], axis=0)


def tendency(along_x, along_y, along_z, state):
    depth_cells, width_cells, cross_cells = (state.shape[1], state.shape[2], state.shape[3])
    rate = -(
        derive(flux(along_x, 0), 2, width_cells)
        + derive(flux(along_y, 1), 3, cross_cells)
        + derive(flux(along_z, 2), 1, depth_cells)
    )
    rate = rate.at[3].add(GRAVITY * state[0])
    rate = rate.at[7].add(GRAVITY * state[3])
    return rate


def line_fields(new_state):
    dens = 0.5 + jax.nn.softplus(new_state[0])
    speed = (COS_VIEW * new_state[3] + SIN_VIEW * new_state[1]) / dens
    field_sq = jnp.sum(new_state[4:7] * new_state[4:7], axis=0)
    source = jax.nn.softplus(new_state[7] - 0.5 * field_sq) / dens
    return jnp.stack([dens, speed, source], axis=1)


def column_shift(level):
    return (1732 * level + 1000) // 2000


def shear(rows, row_shift, depth_cells):
    cells = rows.shape[2]
    tiles = lax.axis_size("tile")
    slabs = lax.axis_size("depth")
    first = [column_shift(d * depth_cells) // cells for d in range(slabs)]
    last = [
        (column_shift((d + 1) * depth_cells - 1) + cells - 1) // cells for d in range(slabs)
    ]
    count = max(high - low + 1 for low, high in zip(first, last))
    pieces = []
    for turn in range(count):
        route = [
            (((t + first[d] + turn) % tiles) * slabs + d, t * slabs + d)
            for t in range(tiles)
            for d in range(slabs)
            if first[d] + turn <= last[d]
        ]
        pieces.append(lax.ppermute(rows, ("tile", "depth"), route))
    joined = jnp.concatenate(pieces, axis=2)
    lowest = lax.axis_index("depth") * depth_cells
    offset = row_shift - column_shift(lowest) // cells * cells
    target = jnp.arange(cells, dtype=jnp.int32)
    anchor = jnp.arange(count * cells, dtype=jnp.int32)
    select = (anchor[None, None, :] == target[None, :, None] + offset[:, None, None]).astype(
        jnp.float32
    )
    return jnp.einsum("lcxa,lwx->lcwa", joined, select, precision=lax.Precision.HIGHEST)


def regroup(rows):
    return lax.all_to_all(rows, "depth", split_axis=3, concat_axis=0, tiled=True)


def emergent(columns):
    positions = columns.shape[0]
    flat = columns.reshape(positions, 3, -1)
    dens = flat[:, 0]
    speed = flat[:, 1]
    source = flat[:, 2]
    waves = (jnp.arange(W, dtype=jnp.float32) - 0.5 * (W - 1)) * SPACING
    gap = waves[:, None, None] - speed[None]
    dtau = 2.0 / positions * dens[None] * (1.0 + STRENGTH * jnp.exp(-gap * gap))
    order = jnp.arange(positions, dtype=jnp.int32)
    earlier = (order[None, :] < order[:, None]).astype(jnp.float32)
    above = jnp.einsum("kj,wjc->wkc", earlier, dtau, precision=lax.Precision.HIGHEST)
    inner = jnp.sum(source[None] * jnp.exp(-above) * (1.0 - jnp.exp(-dtau)), axis=1)
    total = inner + source[-1][None] * jnp.exp(-above[:, -1] - dtau[:, -1])
    return total.reshape((W,) + columns.shape[2:])


def per_device(density, momentum, magnetic, energy, shifts, levels):
    state = jnp.concatenate([density[None], momentum, magnetic, energy[None]], axis=0)
    count_vars, depth_cells, width_cells, cross_cells = state.shape
    depth_at = lax.axis_index("depth")
    slabs = lax.axis_size("depth")
    along_x = padded_2(state, (("tile", 2),), 3, True)
    padded = padded_2(state, (("depth", 1),), 3, False)
    rim_shape = (count_vars, 3, width_cells, cross_cells)
    head = jnp.where(depth_at == 0, jnp.broadcast_to(state[:, :1], rim_shape), padded[:, :3])
    tail = jnp.where(
        depth_at == slabs - 1,
        jnp.broadcast_to(state[:, -1:], rim_shape),
        padded[:, depth_cells + 3 :],
    )
    along_z = jnp.concatenate([head, state, tail], axis=1)
    along_y = jnp.pad(state, ((0, 0), (0, 0), (0, 0), (3, 3)), mode="wrap")
    new_state = state + SECTION * tendency(along_x, along_y, along_z, state)
    fields = line_fields(new_state)
    most = min(MOST, depth_cells)
    lowest = depth_at * depth_cells
    ahead = jnp.sum((levels < lowest).astype(jnp.int32))
    position = jnp.minimum(ahead + jnp.arange(most, dtype=jnp.int32), levels.shape[0] - 1)
    held = jnp.clip(levels[position] - lowest, 0, depth_cells - 1)
    sheared = shear(fields[held], shifts[position], depth_cells)
    slab = levels // depth_cells
    before = jnp.sum((levels[None, :] < (slab * depth_cells)[:, None]).astype(jnp.int32), axis=1)
    rank = jnp.arange(levels.shape[0], dtype=jnp.int32) - before
    columns = regroup(sheared)[slab * most + rank]
    intensity = emergent(columns)
    return (new_state, intensity)


def solution(mesh):
    return jax.shard_map(
        per_device,
        mesh=mesh,
        in_specs=(
            P("depth", "tile", None),
            P(None, "depth", "tile", None),
            P(None, "depth", "tile", None),
            P("depth", "tile", None),
            P(),
            P(),
        ),
        out_specs=(P(None, "depth", "tile", None), P(None, "tile", "depth")),
        check_vma=False,
    )
```

profile of v0, /device:TPU:27, one launch (start us, length us, event | category | flops | bytes accessed | tf_op | source)
XLA Modules:
  0.0 83.1 jit_solution(17729562352915992667)
XLA Ops:
  0.6 1.3 %pad_maximum_fusion.4 = f32[8,16,16,128]{3,2,1,0:T(8,128)S(1)} fusion(f32[1,16,16,128]{3,2,1,0:T(8,128)} %bitcast.166, f32[3,16,16,128]{3,2,1,0:T(8,128)} %param.18, f32[3,16,16,128]{3,2,1,0:T(8,128)} %param.17, f32[1,16,16,128]{3,2,1,0:T(8,128)} %bitcast.152), kind=kLoop, calls=%fused_computation.75 | loop fusion | flops 786432 | bytes 2097152 | tf_op jit(solution)/shard_map/concatenate | solution.py:144
  1.9 0.8 fusion.86
  2.7 2.6 %collective-permute-start.3 = (f32[8,3,16,128]{3,2,1,0:T(8,128)}, f32[8,3,16,128]{3,2,1,0:T(8,128)}, u32[]{:S(2)}, u32[]{:S(2)}) collective-permute-start(f32[8,3,16,128]{3,2,1,0:T(8,128)} %get-tuple-element.116), channel_id=1, source_target_pairs={{1,0},{2,1},{3,2},{5,4},{6,5},{7,6},{9,8},{10,9},{11,10},{13,12},{... | collective-permute-start | bytes 589832 | tf_op jit(solution)/shard_map/ppermute | solution.py:35
  5.3 3.0 %collective-permute-start.2 = (f32[8,3,16,128]{3,2,1,0:T(8,128)}, f32[8,3,16,128]{3,2,1,0:T(8,128)}, u32[]{:S(2)}, u32[]{:S(2)}) collective-permute-start(f32[8,3,16,128]{3,2,1,0:T(8,128)} %get-tuple-element.115), channel_id=1, source_target_pairs={{0,1},{1,2},{2,3},{4,5},{5,6},{6,7},{8,9},{9,10},{10,11},{12,13},{... | collective-permute-start | bytes 589832 | tf_op jit(solution)/shard_map/ppermute | solution.py:33
  8.3 0.9 %fusion.84 = (f32[8,16,3,128]{3,2,1,0:T(4,128)}, f32[8,16,3,128]{3,2,1,0:T(4,128)}) fusion(f32[8,16,16,128]{3,2,1,0:T(8,128)S(1)} %pad_maximum_fusion.4), kind=kLoop, calls=%fused_computation.197 | loop fusion | bytes 786432 | tf_op jit(solution)/shard_map/slice | solution.py:30
  9.5 3.9 %collective-permute-start = (f32[8,16,3,128]{3,2,1,0:T(4,128)}, f32[8,16,3,128]{3,2,1,0:T(4,128)}, u32[]{:S(2)}, u32[]{:S(2)}) collective-permute-start(f32[8,16,3,128]{3,2,1,0:T(4,128)} %get-tuple-element.109), channel_id=1, source_target_pairs={{0,4},{4,8},{8,12},{12,16},{16,20},{20,24},{24,28},{28,0},{1,5},{5... | collective-permute-start | bytes 589832 | tf_op jit(solution)/shard_map/ppermute | solution.py:33
  13.5 0.3 fusion.85
  13.9 0.6 copy-done.2
  14.6 1.1 %maximum_bitcast_fusion = (f32[16,16,134]{2,1,0:T(8,128)}, f32[1,16,16,134]{3,2,1,0:T(8,128)}) fusion(f32[8,16,16,3]{3,2,1,0:T(8,128)S(1)} %get-tuple-element.112, f32[8,16,16,3]{3,2,1,0:T(8,128)S(1)} %get-tuple-element.111, f32[1,16,16,128]{3,2,1,0:T(8,128)S(1)} %bitcast.167, f32[3,16,16,128]{3,2,1,0:T(8,128)S(1)} %copy-done.3, ...), kind=kLoop, calls=%fused_computation.110 | loop fusion | flops 343040 | bytes 1372160 | tf_op jit(solution)/shard_map/div | solution.py:57
  15.7 2.2 %pad_maximum_fusion = f32[8,16,16,134]{3,2,1,0:T(8,128)} fusion(f32[8,16,16,3]{3,2,1,0:T(8,128)S(1)} %get-tuple-element.112, f32[1,16,16,128]{3,2,1,0:T(8,128)S(1)} %bitcast.168, f32[3,16,16,128]{3,2,1,0:T(8,128)S(1)} %copy-done.3, f32[3,16,16,128]{3,2,1,0:T(8,128)S(1)} %copy-done.2, f32[1,16,16,128]{3,2,1,0:T(8,128)S(1)} %bitcast.154, ...), kind=kLoop, calls=%fused_computation.22 | loop fusion | flops 1372160 | bytes 2195456 | tf_op jit(solution)/shard_map/jit(_pad)/concatenate | solution.py:158
  17.9 2.7 %multiply_reduce_fusion.3 = (f32[16,16,134]{2,1,0:T(8,128)}, f32[16,16,134]{2,1,0:T(8,128)}, f32[16,16,134]{2,1,0:T(8,128)}, f32[3,16,16,134]{3,2,1,0:T(8,128)S(1)}) fusion(f32[8,16,16,134]{3,2,1,0:T(8,128)} %pad_maximum_fusion, f32[16,16,134]{2,1,0:T(8,128)} %get-tuple-element.94), kind=kLoop, calls=%fused_computation.80 | loop fusion | flops 617472 | bytes 1783808 | tf_op jit(solution)/shard_map/reduce_sum | solution.py:59
  20.6 0.9 %copy-done.6 = f32[3,16,16,134]{3,2,1,0:T(8,128)} copy-done((f32[3,16,16,134]{3,2,1,0:T(8,128)}, f32[3,16,16,134]{3,2,1,0:T(8,128)S(1)}, u32[]{:S(2)}) %copy-start.6) | copy-done | bytes 411672
  21.5 0.7 slice_bitcast_fusion
  22.2 1.2 %broadcast_multiply_fusion = (s32[24]{0:T(128)}, s32[24]{0:T(128)}, s32[]{:T(128)}) fusion(s32[24]{0:T(128)S(1)} %copy-done.1, s32[]{:T(128)S(6)} %mul.475), kind=kLoop, calls=%fused_computation.192 | loop fusion | flops 455 | bytes 296 | tf_op jit(solution)/shard_map/mul | solution.py:168
  23.4 0.6 fusion.79
  24.1 0.6 gather_fusion.1
  24.8 1.2 %gather_fusion = s32[8]{0:T(128)} fusion(s32[24]{0:T(128)S(1)} %copy-done, s32[1024]{0:T(1024)S(1)} %pad_clamp_fusion.2), kind=kCustom, calls=%fused_computation | custom fusion | bytes 96 | tf_op jit(solution)/shard_map/gather | solution.py:166
  26.0 1.4 %convert_reduce_fusion = s32[24]{0:T(128)} fusion(s32[24]{0:T(128)S(1)} %copy-done.1, s32[24]{0:T(128)} %get-tuple-element.83), kind=kLoop, calls=%fused_computation.172 | loop fusion | flops 1704 | bytes 288 | tf_op jit(solution)/shard_map/reduce_sum | solution.py:168
  27.4 2.1 %multiply_subtract_fusion = (f32[3,16,16,134]{3,2,1,0:T(8,128)S(1)}, f32[3,16,16,134]{3,2,1,0:T(8,128)S(1)}) fusion(f32[3,16,16,134]{3,2,1,0:T(8,128)} %copy-done.6, f32[8,16,16,134]{3,2,1,0:T(8,128)} %pad_maximum_fusion, f32[16,16,134]{2,1,0:T(8,128)} %bitcast.184, f32[16,16,134]{2,1,0:T(8,128)} %slice_bitcast_fusion), kind=kLoop, calls=%fused_computation.78 | loop fusion | flops 617472 | bytes 2332672 | tf_op jit(solution)/shard_map/sub | solution.py:64
  29.8 0.7 copy-done.8
  30.6 1.1 %fusion.53 = f32[1,16,16,134]{3,2,1,0:T(8,128)S(1)} fusion(f32[1,16,16,134]{3,2,1,0:T(8,128)S(1)} %copy-done.8, f32[16,16,134]{2,1,0:T(8,128)S(1)} %copy-done.11, f32[1,16,16,134]{3,2,1,0:T(8,128)S(1)} %get-tuple-element.89, f32[3,16,16,134]{3,2,1,0:T(8,128)} %copy-done.6, f32[16,16,134]{2,1,0:T(8,128)S(1)} %copy-done.10, f32[16,16,134]{2,1,0:T(8,128)S(1)} %copy-done.9), kind=kLoop, calls=%fused_computation.112 | loop fusion | flops 343040 | bytes 960512 | tf_op jit(solution)/shard_map/sub | solution.py:65
  31.7 0.3 fusion.6
  32.1 0.9 %broadcast_select_fusion = f32[8,3,16,128]{3,2,1,0:T(8,128)S(1)} fusion(f32[8,3,16,128]{3,2,1,0:T(8,128)} %collective-permute-done.3, f32[8,16,128]{2,1,0:T(8,128)S(1)} %get-tuple-element.114, pred[]{:T(512)S(6)} %eq.20), kind=kLoop, calls=%fused_computation.159 | loop fusion | flops 49152 | bytes 458753 | tf_op jit(solution)/shard_map/jit(_where)/select_n | solution.py:152
  33.0 1.0 %broadcast_select_fusion.1 = f32[8,3,16,128]{3,2,1,0:T(8,128)S(1)} fusion(f32[8,3,16,128]{3,2,1,0:T(8,128)} %collective-permute-done.2, f32[8,16,128]{2,1,0:T(8,128)S(1)} %get-tuple-element.113, pred[]{:T(512)S(6)} %eq.19), kind=kLoop, calls=%fused_computation.160 | loop fusion | flops 49152 | bytes 458753 | tf_op jit(solution)/shard_map/jit(_where)/select_n | solution.py:151
  34.4 0.8 %maximum_bitcast_fusion.1 = (f32[16,22,128]{2,1,0:T(8,128)S(1)}, f32[1,16,22,128]{3,2,1,0:T(8,128)S(1)}) fusion(f32[8,16,3,128]{3,2,1,0:T(4,128)S(1)} %collective-permute-done.1, f32[8,16,3,128]{3,2,1,0:T(4,128)} %collective-permute-done, f32[1,16,16,128]{3,2,1,0:T(8,128)S(1)} %bitcast.173, f32[3,16,16,128]{3,2,1,0:T(8,128)S(1)} %copy-done.3, ...), kind=kLoop, calls=%fused_computation.122 | loop fusion | flops 450560 | bytes 1802240 | tf_op jit(solution)/shard_map/div | solution.py:57
  35.2 1.2 %pad_maximum_fusion.1 = f32[8,16,22,128]{3,2,1,0:T(8,128)S(1)} fusion(f32[8,16,3,128]{3,2,1,0:T(4,128)S(1)} %collective-permute-done.1, f32[1,16,16,128]{3,2,1,0:T(8,128)S(1)} %bitcast.174, f32[3,16,16,128]{3,2,1,0:T(8,128)S(1)} %copy-done.3, f32[3,16,16,128]{3,2,1,0:T(8,128)S(1)} %copy-done.2, f32[1,16,16,128]{3,2,1,0:T(8,128)S(1)} %bitcast.160, ...), kind=kLoop, calls=%fused_computation.36 | loop fusion | flops 1802240 | bytes 2883584 | tf_op jit(solution)/shard_map/concatenate | solution.py:31
  37.1 0.9 %fusion.55 = (f32[3,16,22,128]{3,2,1,0:T(8,128)S(1)}, f32[1,16,22,128]{3,2,1,0:T(8,128)S(1)}) fusion(f32[3,16,22,128]{3,2,1,0:T(8,128)S(1)} %get-tuple-element.99, f32[16,22,128]{2,1,0:T(8,128)S(1)} %get-tuple-element.81, f32[16,22,128]{2,1,0:T(8,128)S(1)} %get-tuple-element.76, f32[8,16,3,128]{3,2,1,0:T(4,128)S(1)} %collective-permute-done.1, ...), kind=kLoop, calls=%fused_computation.120 | loop fusion | flops 540672 | bytes 2490368 | tf_op jit(solution)/shard_map/scatter-add | solution.py:63
  38.3 1.1 %fusion.15 = f32[8,16,22,128]{3,2,1,0:T(8,128)S(1)} fusion(f32[8,16,3,128]{3,2,1,0:T(4,128)S(1)} %collective-permute-done.1, f32[8,16,3,128]{3,2,1,0:T(4,128)} %collective-permute-done, f32[1,16,16,128]{3,2,1,0:T(8,128)S(1)} %bitcast.178, f32[3,16,16,128]{3,2,1,0:T(8,128)S(1)} %copy-done.3, f32[3,16,16,128]{3,2,1,0:T(8,128)S(1)} %copy-done.2, ...), kind=kLoop, calls=%fused_computation.27 | loop fusion | flops 5046272 | bytes 4145152 | tf_op jit(solution)/shard_map/concatenate | solution.py:66
  39.4 1.6 %fusion.33 = f32[8,16,16,128]{3,2,1,0:T(8,128)S(1)} fusion(f32[8,22,16,128]{3,2,1,0:T(8,128)S(1)} %fusion.24, f32[8,16,16,134]{3,2,1,0:T(8,128)S(1)} %fusion.6, f32[8,16,22,128]{3,2,1,0:T(8,128)S(1)} %fusion.15), kind=kLoop, calls=%fused_computation.54 | loop fusion | flops 6553600 | bytes 19922944 | tf_op jit(solution)/shard_map/neg | solution.py:71
  41.5 0.6 gather_fusion.2
  42.0 1.9 %collective-permute-start.6 = (f32[8,3,16,128]{3,2,1,0:T(8,128)S(1)}, f32[8,3,16,128]{3,2,1,0:T(8,128)S(1)}, u32[]{:S(2)}, u32[]{:S(2)}) collective-permute-start(f32[8,3,16,128]{3,2,1,0:T(8,128)S(1)} %gather_fusion.2), channel_id=1, source_target_pairs={{9,1},{14,2},{19,3},{13,5},{18,6},{23,7},{17,9},{22,10},{27,11},{2... | collective-permute-start | bytes 589832 | tf_op jit(solution)/shard_map/ppermute | solution.py:110
  44.0 0.7 collective-permute-start.4
  44.8 5.8 %collective-permute-done.6 = f32[8,3,16,128]{3,2,1,0:T(8,128)S(1)} collective-permute-done((f32[8,3,16,128]{3,2,1,0:T(8,128)S(1)}, f32[8,3,16,128]{3,2,1,0:T(8,128)S(1)}, u32[]{:S(2)}, u32[]{:S(2)}) %collective-permute-start.6) | collective-permute-done | bytes 196640 | tf_op jit(solution)/shard_map/ppermute | solution.py:110
  50.6 1.7 %collective-permute-done.5 = f32[8,3,16,128]{3,2,1,0:T(8,128)S(1)} collective-permute-done((f32[8,3,16,128]{3,2,1,0:T(8,128)S(1)}, f32[8,3,16,128]{3,2,1,0:T(8,128)S(1)}, u32[]{:S(2)}, u32[]{:S(2)}) %collective-permute-start.5) | collective-permute-done | bytes 196640 | tf_op jit(solution)/shard_map/ppermute | solution.py:110
  52.2 0.3 convolution_bitcast_fusion.1
  52.6 0.5 copy.30
  53.2 1.2 %reshape.539 = f32[4,1,12288]{2,1,0:T(1,128)} reshape(f32[128,3,8,16]{3,2,1,0:T(8,128)S(1)} %bitcast.180) | data formatting | bytes 393216
  54.4 12.1 %all-to-all-start = ((f32[4,1,12288]{2,1,0:T(1,128)}), f32[4,1,12288]{2,1,0:T(1,128)S(1)}, u32[]{:S(2)}, u32[]{:S(2)}) async-start(f32[4,1,12288]{2,1,0:T(1,128)} %reshape.539), calls=%async_computation | async-start | bytes 393216 | tf_op jit(solution)/shard_map/all_to_all | solution.py:123
  66.5 5.3 %all-to-all-done = f32[4,1,12288]{2,1,0:T(1,128)S(1)} async-done(((f32[4,1,12288]{2,1,0:T(1,128)}), f32[4,1,12288]{2,1,0:T(1,128)S(1)}, u32[]{:S(2)}, u32[]{:S(2)}) %all-to-all-start) | async-done | bytes 196640 | tf_op jit(solution)/shard_map/all_to_all | solution.py:123
  71.9 0.5 broadcast.494
  72.4 1.2 %reduce.16 = f32[4,12288]{1,0:T(4,128)S(1)} reduce(f32[4,1,12288]{2,1,0:T(1,128)S(1)} %all-to-all-done, f32[]{:T(128)} %broadcast.494), dimensions={1}, to_apply=%all_to_all.13.reduce_sub_computation | reduce | bytes 393220 | tf_op jit(solution)/shard_map/all_to_all | solution.py:123
  73.6 0.5 reshape.540
  74.1 0.6 copy.36
  74.7 0.6 gather_fusion.3
  75.3 0.3 reshape.530
  75.8 4.4 %fusion.3 = (f32[48,24,512]{2,1,0:T(8,128)S(1)}, f32[48,512]{1,0:T(8,128)S(1)}, f32[48,24,512]{2,1,0:T(8,128)}) fusion(f32[24,512]{1,0:T(8,128)S(1)} %get-tuple-element.124, f32[48]{0:T(128)S(1)} %add_multiply_fusion, f32[24,512]{1,0:T(8,128)S(1)} %get-tuple-element.125, f32[24,512]{1,0:T(8,128)S(1)} %bitcast.187), kind=kOutput, calls=%fused_computation.8 | convolution fusion | flops 180462144 | bytes 4964544 | tf_op jit(solution)/shard_map/kj,wjc->wkc/dot_general | solution.py:137
  80.3 1.6 %fusion.70 = f32[48,512]{1,0:T(8,128)S(1)} fusion(f32[48,24,512]{2,1,0:T(8,128)S(1)} %get-tuple-element.120, f32[48,24,512]{2,1,0:T(8,128)} %get-tuple-element.123), kind=kLoop, calls=%fused_computation.161 | loop fusion | flops 49152 | bytes 294912 | tf_op jit(solution)/shard_map/exp | solution.py:139
  82.2 0.9 %copy.34 = f32[48,16,32]{0,2,1:T(8,128)} copy(f32[48,16,32]{2,1,0:T(8,128)S(1)} %multiply_add_fusion.1) | data formatting | bytes 196608
  (71 shorter events, 3.4 us)
Async XLA Ops:
  0.6 24.1 %copy-start = (s32[24]{0:T(128)S(1)}, s32[24]{0:T(128)}, u32[]{:S(2)}) copy-start(s32[24]{0:T(128)} %param.20) | copy-start | bytes 292
  2.7 29.3 %collective-permute-start.3 = (f32[8,3,16,128]{3,2,1,0:T(8,128)}, f32[8,3,16,128]{3,2,1,0:T(8,128)}, u32[]{:S(2)}, u32[]{:S(2)}) collective-permute-start(f32[8,3,16,128]{3,2,1,0:T(8,128)} %get-tuple-element.116), channel_id=1, source_target_pairs={{1,0},{2,1},{3,2},{5,4},{6,5},{7,6},{9,8},{10,9},{11,10},{13,12},{... | collective-permute-start | bytes 589832 | tf_op jit(solution)/shard_map/ppermute | solution.py:35
  5.3 27.7 %collective-permute-start.2 = (f32[8,3,16,128]{3,2,1,0:T(8,128)}, f32[8,3,16,128]{3,2,1,0:T(8,128)}, u32[]{:S(2)}, u32[]{:S(2)}) collective-permute-start(f32[8,3,16,128]{3,2,1,0:T(8,128)} %get-tuple-element.115), channel_id=1, source_target_pairs={{0,1},{1,2},{2,3},{4,5},{5,6},{6,7},{8,9},{9,10},{10,11},{12,13},{... | collective-permute-start | bytes 589832 | tf_op jit(solution)/shard_map/ppermute | solution.py:33
  9.3 25.1 %collective-permute-start.1 = (f32[8,16,3,128]{3,2,1,0:T(4,128)}, f32[8,16,3,128]{3,2,1,0:T(4,128)S(1)}, u32[]{:S(2)}, u32[]{:S(2)}) collective-permute-start(f32[8,16,3,128]{3,2,1,0:T(4,128)} %get-tuple-element.110), channel_id=1, source_target_pairs={{4,0},{8,4},{12,8},{16,12},{20,16},{24,20},{28,24},{0,28},{5,1},{9... | collective-permute-start | bytes 589832 | tf_op jit(solution)/shard_map/ppermute | solution.py:35
  9.5 24.8 %collective-permute-start = (f32[8,16,3,128]{3,2,1,0:T(4,128)}, f32[8,16,3,128]{3,2,1,0:T(4,128)}, u32[]{:S(2)}, u32[]{:S(2)}) collective-permute-start(f32[8,16,3,128]{3,2,1,0:T(4,128)} %get-tuple-element.109), channel_id=1, source_target_pairs={{0,4},{4,8},{8,12},{12,16},{16,20},{20,24},{24,28},{28,0},{1,5},{5... | collective-permute-start | bytes 589832 | tf_op jit(solution)/shard_map/ppermute | solution.py:33
  13.4 1.0 %copy-start.2 = (f32[3,16,16,128]{3,2,1,0:T(8,128)S(1)}, f32[3,16,16,128]{3,2,1,0:T(8,128)}, u32[]{:S(2)}) copy-start(f32[3,16,16,128]{3,2,1,0:T(8,128)} %param.17) | copy-start | bytes 1179652
  13.5 1.1 %copy-start.3 = (f32[3,16,16,128]{3,2,1,0:T(8,128)S(1)}, f32[3,16,16,128]{3,2,1,0:T(8,128)}, u32[]{:S(2)}) copy-start(f32[3,16,16,128]{3,2,1,0:T(8,128)} %param.18) | copy-start | bytes 1179652
  13.5 1.1 %copy-start.4 = (f32[16,16,128]{2,1,0:T(8,128)S(1)}, f32[16,16,128]{2,1,0:T(8,128)}, u32[]{:S(2)}) copy-start(f32[16,16,128]{2,1,0:T(8,128)} %param.16) | copy-start | bytes 393220
  13.5 1.2 %copy-start.5 = (f32[16,16,128]{2,1,0:T(8,128)S(1)}, f32[16,16,128]{2,1,0:T(8,128)}, u32[]{:S(2)}) copy-start(f32[16,16,128]{2,1,0:T(8,128)} %param.19) | copy-start | bytes 393220
  17.9 4.3 %copy-start.1 = (s32[24]{0:T(128)S(1)}, s32[24]{0:T(128)}, u32[]{:S(2)}) copy-start(s32[24]{0:T(128)} %param.21) | copy-start | bytes 292
  20.6 0.9 %copy-start.6 = (f32[3,16,16,134]{3,2,1,0:T(8,128)}, f32[3,16,16,134]{3,2,1,0:T(8,128)S(1)}, u32[]{:S(2)}) copy-start(f32[3,16,16,134]{3,2,1,0:T(8,128)S(1)} %get-tuple-element.90) | copy-start | bytes 1234948
  27.4 2.1 %copy-start.9 = (f32[16,16,134]{2,1,0:T(8,128)S(1)}, f32[16,16,134]{2,1,0:T(8,128)}, u32[]{:S(2)}) copy-start(f32[16,16,134]{2,1,0:T(8,128)} %get-tuple-element.74) | copy-start | bytes 411652
  27.4 2.2 %copy-start.10 = (f32[16,16,134]{2,1,0:T(8,128)S(1)}, f32[16,16,134]{2,1,0:T(8,128)}, u32[]{:S(2)}) copy-start(f32[16,16,134]{2,1,0:T(8,128)} %get-tuple-element.78) | copy-start | bytes 411652
  29.5 1.0 %copy-start.8 = (f32[1,16,16,134]{3,2,1,0:T(8,128)S(1)}, f32[1,16,16,134]{3,2,1,0:T(8,128)}, u32[]{:S(2)}) copy-start(f32[1,16,16,134]{3,2,1,0:T(8,128)} %get-tuple-element.95) | copy-start | bytes 411652
  29.5 1.0 %copy-start.11 = (f32[16,16,134]{2,1,0:T(8,128)S(1)}, f32[16,16,134]{2,1,0:T(8,128)}, u32[]{:S(2)}) copy-start(f32[16,16,134]{2,1,0:T(8,128)} %get-tuple-element.75) | copy-start | bytes 411652
  29.8 1.9 %copy-start.13 = (s32[8]{0:T(128)S(1)}, s32[8]{0:T(128)}, u32[]{:S(2)}) copy-start(s32[8]{0:T(128)} %gather_fusion) | copy-start | bytes 100
  41.2 11.4 %copy-start.7 = (f32[8,16,16,128]{3,2,1,0:T(8,128)}, f32[8,16,16,128]{3,2,1,0:T(8,128)S(1)}, u32[]{:S(2)}) copy-start(f32[8,16,16,128]{3,2,1,0:T(8,128)S(1)} %multiply_add_fusion) | copy-start | bytes 3145732
  41.2 3.5 %copy-start.12 = (s32[24]{0:T(128)S(1)}, s32[24]{0:T(128)}, u32[]{:S(2)}) copy-start(s32[24]{0:T(128)} %get-tuple-element.84) | copy-start | bytes 292
  41.2 3.5 %copy-start.14 = (s32[24]{0:T(128)S(1)}, s32[24]{0:T(128)}, u32[]{:S(2)}) copy-start(s32[24]{0:T(128)} %convert_reduce_fusion) | copy-start | bytes 292
  42.0 8.5 %collective-permute-start.6 = (f32[8,3,16,128]{3,2,1,0:T(8,128)S(1)}, f32[8,3,16,128]{3,2,1,0:T(8,128)S(1)}, u32[]{:S(2)}, u32[]{:S(2)}) collective-permute-start(f32[8,3,16,128]{3,2,1,0:T(8,128)S(1)} %gather_fusion.2), channel_id=1, source_target_pairs={{9,1},{14,2},{19,3},{13,5},{18,6},{23,7},{17,9},{22,10},{27,11},{2... | collective-permute-start | bytes 589832 | tf_op jit(solution)/shard_map/ppermute | solution.py:110
  44.0 8.3 %collective-permute-start.5 = (f32[8,3,16,128]{3,2,1,0:T(8,128)S(1)}, f32[8,3,16,128]{3,2,1,0:T(8,128)S(1)}, u32[]{:S(2)}, u32[]{:S(2)}) collective-permute-start(f32[8,3,16,128]{3,2,1,0:T(8,128)S(1)} %gather_fusion.2), channel_id=1, source_target_pairs={{4,0},{5,1},{10,2},{15,3},{8,4},{9,5},{14,6},{19,7},{12,8},{13,9},... | collective-permute-start | bytes 589832 | tf_op jit(solution)/shard_map/ppermute | solution.py:110
  44.0 8.2 %collective-permute-start.4 = (f32[8,3,16,128]{3,2,1,0:T(8,128)S(1)}, f32[8,3,16,128]{3,2,1,0:T(8,128)S(1)}, u32[]{:S(2)}, u32[]{:S(2)}) collective-permute-start(f32[8,3,16,128]{3,2,1,0:T(8,128)S(1)} %gather_fusion.2), channel_id=1, source_target_pairs={{0,0},{1,1},{6,2},{11,3},{4,4},{5,5},{10,6},{15,7},{8,8},{9,9},{14... | collective-permute-start | bytes 589832 | tf_op jit(solution)/shard_map/ppermute | solution.py:110
  54.4 17.5 %all-to-all-start = ((f32[4,1,12288]{2,1,0:T(1,128)}), f32[4,1,12288]{2,1,0:T(1,128)S(1)}, u32[]{:S(2)}, u32[]{:S(2)}) async-start(f32[4,1,12288]{2,1,0:T(1,128)} %reshape.539), calls=%async_computation | async-start | bytes 393216 | tf_op jit(solution)/shard_map/all_to_all | solution.py:123
where the time goes:
time: 83.8 us; the launch traced here: 83.1 us
  other arithmetic  26.4 us (32%)
  starting transfers between devices  24.6 us (29%)
  local copies, waits for them, and re-layouts  13.4 us (16%)
  waiting for transfers between devices  12.8 us (15%)
  matrix products  4.72 us (6%)
  between operations  1.15 us (1%)
    all_to_all x1, starting transfers between devices, regroup(): lax.all_to_all(rows, 'depth', split_axis=3, concat_axis=0, tiled=True)  12.1 us
    ppermute x3, waiting for transfers between devices, shear(): pieces.append(lax.ppermute(rows, ('tile', 'depth'), route))  7.49 us
    ppermute x2, starting transfers between devices, padded_2(): lax.ppermute(tail, axis, [(i, (i + 1) % count) for i in range(ends)])  6.95 us
    all_to_all x1, waiting for transfers between devices, regroup(): lax.all_to_all(rows, 'depth', split_axis=3, concat_axis=0, tiled=True)  5.33 us
    unnamed x35, local copies, waits for them, and re-layouts  5.16 us
    dot_general x1, matrix products, emergent(): jnp.einsum('kj,wjc->wkc', earlier, dtau, precision=lax.Precision.HIGHEST)  4.38 us
    reduce_sum x3, other arithmetic, flux(): jnp.sum(moment * velocity, axis=0)  3.04 us
    ppermute x2, starting transfers between devices, padded_2(): lax.ppermute(head, axis, [((i + 1) % count, i) for i in range(ends)])  2.83 us
  transfers between devices with their start and end apart: 8, of which 3 were waited for; matrix products, arithmetic and copies ran while one was open for 23% of the time, Pallas kernels for 0%

commit v1 on v0

v1 whole, which is shorter than its diff:
```python
import functools
import math

import jax
import jax.numpy as jnp
from jax import lax
from jax.experimental import pallas as pl
from jax.experimental.pallas import tpu as pltpu
from jax.sharding import PartitionSpec as P

W = 48
MOST = 8
GAMMA = 5.0 / 3.0
SECTION = 0.02
GRAVITY = 0.5
SIN_VIEW = 0.8660254037844386
COS_VIEW = 0.5
STRENGTH = 4.0
SPACING = 0.25
LOG2E = 1.4426950408889634
ROOT_LOG2E = math.sqrt(LOG2E)
F32 = jnp.float32
MESH = pl.DeviceIdType.MESH
PAD = 8


def column_shift(level):
    return (1732 * level + 1000) // 2000


def softplus(a):
    return jnp.maximum(a, 0.0) + jnp.log1p(jnp.exp(-jnp.abs(a)))


class Plan:
    def __init__(self, tiles, slabs, depth_cells, width, cross, positions):
        self.tiles, self.slabs = tiles, slabs
        self.depth_cells, self.width, self.cross = depth_cells, width, cross
        self.positions = positions
        self.most = min(MOST, depth_cells)
        self.lanes = cross // slabs
        self.blocks = 128 // self.lanes
        self.items = 3 * self.most
        self.packed = -(-self.items // self.blocks)
        self.low = [column_shift(d * depth_cells) for d in range(slabs)]
        high = [column_shift((d + 1) * depth_cells - 1) for d in range(slabs)]
        self.window = max(h - l for l, h in zip(self.low, high)) + width
        self.rows = -(-self.window // 8) * 8
        self.pieces = []
        for d in range(slabs):
            mine = []
            reach = high[d] - self.low[d] + width
            for o in range(self.low[d] // width, (high[d] + width - 1) // width + 1):
                first = max(0, self.low[d] - width * o)
                last = min(width, self.low[d] + reach - width * o)
                if last > first:
                    mine.append((o, first, last - first, width * o + first - self.low[d]))
            self.pieces.append(mine)
        self.count = max(len(p) for p in self.pieces)


def section_kernel(
    plan, levels, density, momentum, magnetic, energy, state_out, lines_out,
    st, xf, zf, part, ns, pack, recv,
    in_sem, xs_sem, xr_sem, zs_sem, zr_sem, ls_sem, lr_sem, out_sem,
):
    tiles, slabs, cells, width = plan.tiles, plan.slabs, plan.depth_cells, plan.width
    t = lax.axis_index("tile")
    d = lax.axis_index("depth")
    right = lax.rem(t + 1, tiles)
    left = lax.rem(t + tiles - 1, tiles)

    loads = [
        pltpu.make_async_copy(density, st.at[0], in_sem.at[0]),
        pltpu.make_async_copy(momentum, st.at[1:4], in_sem.at[1]),
        pltpu.make_async_copy(magnetic, st.at[4:7], in_sem.at[2]),
        pltpu.make_async_copy(energy, st.at[7], in_sem.at[3]),
    ]
    for load in loads:
        load.start()

    barrier = pltpu.get_barrier_semaphore()

    def greet(tile, depth):
        pl.semaphore_signal(barrier, inc=1, device_id=(tile, depth), device_id_type=MESH)

    greet(right, d)
    greet(left, d)

    @pl.when(d > 0)
    def _():
        greet(t, d - 1)

    @pl.when(d < slabs - 1)
    def _():
        greet(t, d + 1)

    for source in range(slabs):
        for o, _, _, _ in plan.pieces[source]:
            tile = lax.rem(t + o, tiles)
            if o % tiles == 0:

                @pl.when(d != source)
                def _():
                    greet(tile, source)

            else:
                greet(tile, source)

    for load in loads:
        load.wait()

    scale = SECTION / 60.0

    def fluxes(level, carry):
        rho = st[0, level]
        mx, my, mz = st[1, level], st[2, level], st[3, level]
        bx, by, bz = st[4, level], st[5, level], st[6, level]
        en = st[7, level]
        inv = 1.0 / rho
        vx, vy, vz = mx * inv, my * inv, mz * inv
        half_sq = 0.5 * (bx * bx + by * by + bz * bz)
        kinetic = 0.5 * (mx * vx + my * vy + mz * vz)
        total = (GAMMA - 1.0) * (en - kinetic - half_sq) + half_sq
        vb = vx * bx + vy * by + vz * bz
        enthalpy = en + total
        txy = mx * vy - bx * by
        txz = mx * vz - bx * bz
        tyz = my * vz - by * bz
        exy = vx * by - bx * vy
        exz = vx * bz - bx * vz
        eyz = vy * bz - by * vz
        along_x = (
            mx, mx * vx + total - bx * bx, txy, txz, exy, exz, enthalpy * vx - bx * vb
        )
        along_y = (
            my, txy, my * vy + total - by * by, tyz, -exy, eyz, enthalpy * vy - by * vb
        )
        along_z = (
            mz, txz, tyz, mz * vz + total - bz * bz, -exz, -eyz, enthalpy * vz - bz * vb
        )
        for c in range(7):
            xf[c, level, PAD:PAD + width, :] = along_x[c]
            zf[c, level + 3] = along_z[c]

        def cross(f):
            def at(step):
                return pltpu.roll(f, (-step) % plan.cross, 1)

            return (
                45.0 * (at(1) - at(-1)) - 9.0 * (at(2) - at(-2)) + (at(3) - at(-3))
            ) * scale

        base = (
            rho, mx, my, mz + (SECTION * GRAVITY) * rho, bx, by, bz,
            en + (SECTION * GRAVITY) * mz,
        )
        rows_y = (0, 1, 2, 3, 4, 6, 7)
        for c, row in enumerate(rows_y):
            part[row, level] = base[row] - cross(along_y[c])
        part[5, level] = base[5]
        return carry

    lax.fori_loop(0, cells, fluxes, 0)

    targets = 2 + jnp.where(d > 0, 1, 0) + jnp.where(d < slabs - 1, 1, 0)
    for source in range(slabs):
        mine = sum(slabs - (1 if o % tiles == 0 else 0) for o, _, _, _ in plan.pieces[source])
        targets = targets + jnp.where(d == source, mine, 0)
    pl.semaphore_wait(barrier, targets)

    def x_copy(side):
        src = PAD + width - 3 if side == 0 else PAD
        dst = PAD - 3 if side == 0 else PAD + width
        return pltpu.make_async_remote_copy(
            src_ref=xf.at[:, :, pl.ds(src, 3), :],
            dst_ref=xf.at[:, :, pl.ds(dst, 3), :],
            send_sem=xs_sem.at[side],
            recv_sem=xr_sem.at[side],
            device_id=(right if side == 0 else left, d),
            device_id_type=MESH,
        )

    def z_copy(side):
        src = cells if side == 0 else 3
        dst = 0 if side == 0 else cells + 3
        return pltpu.make_async_remote_copy(
            src_ref=zf.at[:, pl.ds(src, 3)],
            dst_ref=zf.at[:, pl.ds(dst, 3)],
            send_sem=zs_sem.at[side],
            recv_sem=zr_sem.at[side],
            device_id=(t, d + 1 if side == 0 else d - 1),
            device_id_type=MESH,
        )

    x_copy(0).start()
    x_copy(1).start()

    @pl.when(d < slabs - 1)
    def _():
        z_copy(0).start()

    @pl.when(d > 0)
    def _():
        z_copy(1).start()

    @pl.when(d == 0)
    def _():
        for c in range(7):
            edge = zf[c, 3]
            for i in range(3):
                zf[c, i] = edge

    @pl.when(d > 0)
    def _():
        z_copy(0).wait_recv()

    @pl.when(d == slabs - 1)
    def _():
        for c in range(7):
            edge = zf[c, cells + 2]
            for i in range(3):
                zf[c, cells + 3 + i] = edge

    @pl.when(d < slabs - 1)
    def _():
        z_copy(1).wait_recv()

    def depth_part(level, carry):
        for c, row in enumerate((0, 1, 2, 3, 4, 5, 7)):
            f = [zf[c, level + i] for i in range(7)]
            part[row, level] = part[row, level] - scale * (
                45.0 * (f[4] - f[2]) - 9.0 * (f[5] - f[1]) + (f[6] - f[0])
            )
        return carry

    lax.fori_loop(0, cells, depth_part, 0)

    x_copy(0).wait_recv()
    x_copy(1).wait_recv()

    def width_part(level, carry):
        for c, row in enumerate((0, 1, 2, 3, 5, 6, 7)):
            f = [xf[c, level, pl.ds(PAD - 3 + i, width), :] for i in range(7)]
            ns[row, level] = part[row, level] - scale * (
                45.0 * (f[4] - f[2]) - 9.0 * (f[5] - f[1]) + (f[6] - f[0])
            )
        ns[4, level] = part[4, level]
        return carry

    lax.fori_loop(0, cells, width_part, 0)

    out_copy = pltpu.make_async_copy(ns, state_out, out_sem.at[0])
    out_copy.start()

    lowest = d * cells
    ahead = jnp.int32(0)
    for k in range(plan.positions):
        ahead = ahead + jnp.where(levels[k] < lowest, 1, 0)
    block_of = lax.broadcasted_iota(jnp.int32, (width, 128), 1) // plan.lanes

    rows = {}
    for slot in range(plan.most):
        held = jnp.clip(
            levels[jnp.minimum(ahead + slot, plan.positions - 1)] - lowest, 0, cells - 1
        )
        dens = 0.5 + softplus(ns[0, held])
        inv = 1.0 / dens
        speed = (COS_VIEW * ns[3, held] + SIN_VIEW * ns[1, held]) * inv
        bx, by, bz = ns[4, held], ns[5, held], ns[6, held]
        source = softplus(ns[7, held] - 0.5 * (bx * bx + by * by + bz * bz)) * inv
        for f, value in enumerate((dens, speed, source)):
            item = 3 * slot + f
            row, block = item // plan.blocks, item % plan.blocks
            for target in range(slabs):
                shift = ((block - target) * plan.lanes) % 128
                moved = pltpu.roll(value, shift, 1) if shift else value
                held_row = rows.get((target, row))
                rows[target, row] = (
                    moved if held_row is None else jnp.where(block_of == block, moved, held_row)
                )
                if block == plan.blocks - 1 or item == plan.items - 1:
                    pack[target, row] = rows.pop((target, row))

    def line_copy(source, n, tile, target):
        _, first, size, at = plan.pieces[source][n]
        return pltpu.make_async_remote_copy(
            src_ref=pack.at[target, :, pl.ds(first, size), :],
            dst_ref=recv.at[source, :, pl.ds(at, size), :],
            send_sem=ls_sem.at[n, target],
            recv_sem=lr_sem.at[source, n],
            device_id=(tile, target),
            device_id_type=MESH,
        )

    def own_copy(source, n):
        _, first, size, at = plan.pieces[source][n]
        return pltpu.make_async_copy(
            pack.at[source, :, pl.ds(first, size), :],
            recv.at[source, :, pl.ds(at, size), :],
            lr_sem.at[source, n],
        )

    for source in range(slabs):

        @pl.when(d == source)
        def _():
            for n, (o, _, _, _) in enumerate(plan.pieces[source]):
                tile = lax.rem(t + tiles - o % tiles, tiles)
                for target in range(slabs):
                    if o % tiles == 0 and target == source:
                        own_copy(source, n).start()
                    else:
                        line_copy(source, n, tile, target).start()

    for source in range(slabs):
        for n, (o, _, _, _) in enumerate(plan.pieces[source]):
            if o % tiles == 0:

                @pl.when(d == source)
                def _():
                    own_copy(source, n).wait()

                @pl.when(d != source)
                def _():
                    line_copy(source, n, left, source).wait_recv()

            else:
                line_copy(source, n, left, source).wait_recv()

    lines_copy = pltpu.make_async_copy(recv, lines_out, out_sem.at[1])
    lines_copy.start()

    x_copy(0).wait_send()
    x_copy(1).wait_send()

    @pl.when(d < slabs - 1)
    def _():
        z_copy(0).wait_send()

    @pl.when(d > 0)
    def _():
        z_copy(1).wait_send()

    for source in range(slabs):

        @pl.when(d == source)
        def _():
            for n, (o, _, _, _) in enumerate(plan.pieces[source]):
                for target in range(slabs):
                    if not (o % tiles == 0 and target == source):
                        line_copy(source, n, left, target).wait_send()

    out_copy.wait()
    lines_copy.wait()


def ray_kernel(
    plan, levels, shifts, lines, state_in, state_out, intensity,
    rows, fields, hold, in_sem, state_sem, out_sem,
):
    slabs, cells, width, blocks = plan.slabs, plan.depth_cells, plan.width, plan.blocks
    lanes, positions = plan.lanes, plan.positions
    lines_copy = pltpu.make_async_copy(lines, rows, in_sem)
    lines_copy.start()
    state_copy = pltpu.make_async_copy(state_in, hold, state_sem)
    state_copy.start()

    slab, slot = [], []
    for k in range(positions):
        level = levels[k]
        slab.append(level // cells)
    run = jnp.int32(0)
    for k in range(positions):
        if k:
            run = jnp.where(slab[k] == slab[k - 1], run + 1, 0)
        slot.append(run)

    lane = lax.broadcasted_iota(jnp.int32, (width, 128), 1)
    within = lax.rem(lane, lanes)
    lines_copy.wait()
    for k in range(positions):
        start = shifts[k] - column_shift(slab[k] * cells)
        got = []
        for f in range(3):
            item = 3 * slot[k] + f
            row, block = item // blocks, lax.rem(item, blocks)
            value = rows[slab[k], row, pl.ds(start, width), :]
            got.append(jnp.take_along_axis(value, within + block * lanes, axis=1))
        dens, speed, source = got
        thin = dens * (-LOG2E * 2.0 / positions)
        fields[0, k] = thin
        fields[1, k] = speed * ROOT_LOG2E
        fields[2, k] = source

    state_copy.wait()
    out_copy = pltpu.make_async_copy(hold, state_out, out_sem)
    out_copy.start()

    groups = W // blocks
    batch = next(b for b in (6, 4, 3, 2, 1) if groups % b == 0)
    which = lax.broadcasted_iota(jnp.int32, (8, 128), 1) // lanes

    for part in range(groups // batch):
        for half in range(width // 8):
            waves = [
                (((part * batch + g) * blocks + which).astype(F32) - 0.5 * (W - 1))
                * (SPACING * ROOT_LOG2E)
                for g in range(batch)
            ]

            def step(k, carry):
                seen, total = carry
                thin = fields[0, k, 8 * half:8 * half + 8, :]
                speed = fields[1, k, 8 * half:8 * half + 8, :]
                source = fields[2, k, 8 * half:8 * half + 8, :]
                strong = STRENGTH * thin
                seen_next, total_next = [], []
                for g in range(batch):
                    gap = waves[g] - speed
                    depth = thin + strong * jnp.exp2(-(gap * gap))
                    after = seen[g] * jnp.exp2(depth)
                    total_next.append(total[g] + source * (seen[g] - after))
                    seen_next.append(after)
                return tuple(seen_next), tuple(total_next)

            ones = tuple(jnp.ones((8, 128), F32) for _ in range(batch))
            zeros = tuple(jnp.zeros((8, 128), F32) for _ in range(batch))
            seen, total = lax.fori_loop(0, positions, step, (ones, zeros), unroll=4)
            last = fields[2, positions - 1, 8 * half:8 * half + 8, :]
            for g in range(batch):
                value = total[g] + last * seen[g]
                for b in range(blocks):
                    intensity[(part * batch + g) * blocks + b, 8 * half:8 * half + 8, :] = value[
                        :, b * lanes:(b + 1) * lanes
                    ]

    out_copy.wait()


def per_device(plan, density, momentum, magnetic, energy, shifts, levels):
    cells, width, cross = density.shape
    slabs = plan.slabs
    any_spec = pl.BlockSpec(memory_space=pl.ANY)
    scalars = pl.BlockSpec(memory_space=pltpu.SMEM)
    state_shape = jax.ShapeDtypeStruct((8, cells, width, cross), F32)
    lines_shape = jax.ShapeDtypeStruct((slabs, plan.packed, plan.rows, 128), F32)
    state, lines = pl.pallas_call(
        functools.partial(section_kernel, plan),
        out_shape=(state_shape, lines_shape),
        in_specs=[scalars] + [any_spec] * 4,
        out_specs=(any_spec, any_spec),
        scratch_shapes=[
            pltpu.VMEM((8, cells, width, cross), F32),
            pltpu.VMEM((7, cells, width + 2 * PAD, cross), F32),
            pltpu.VMEM((7, cells + 6, width, cross), F32),
            pltpu.VMEM((8, cells, width, cross), F32),
            pltpu.VMEM((8, cells, width, cross), F32),
            pltpu.VMEM((slabs, plan.packed, width, 128), F32),
            pltpu.VMEM((slabs, plan.packed, plan.rows, 128), F32),
            pltpu.SemaphoreType.DMA((4,)),
            pltpu.SemaphoreType.DMA((2,)),
            pltpu.SemaphoreType.DMA((2,)),
            pltpu.SemaphoreType.DMA((2,)),
            pltpu.SemaphoreType.DMA((2,)),
            pltpu.SemaphoreType.DMA((plan.count, slabs)),
            pltpu.SemaphoreType.DMA((slabs, plan.count)),
            pltpu.SemaphoreType.DMA((2,)),
        ],
        compiler_params=pltpu.CompilerParams(collective_id=0, has_side_effects=True),
        name="section",
    )(levels, density, momentum, magnetic, energy)
    new_state, intensity = pl.pallas_call(
        functools.partial(ray_kernel, plan),
        out_shape=(state_shape, jax.ShapeDtypeStruct((W, width, plan.lanes), F32)),
        in_specs=[scalars, scalars, any_spec, any_spec],
        out_specs=(any_spec, pl.BlockSpec(memory_space=pltpu.VMEM)),
        scratch_shapes=[
            pltpu.VMEM((slabs, plan.packed, plan.rows, 128), F32),
            pltpu.VMEM((3, plan.positions, width, 128), F32),
            pltpu.VMEM((8, cells, width, cross), F32),
            pltpu.SemaphoreType.DMA,
            pltpu.SemaphoreType.DMA,
            pltpu.SemaphoreType.DMA,
        ],
        name="ray",
    )(levels, shifts, lines, state)
    return new_state, intensity


def solution(mesh):
    tiles, slabs = mesh.shape["tile"], mesh.shape["depth"]

    def body(density, momentum, magnetic, energy, shifts, levels):
        cells, width, cross = density.shape
        plan = Plan(tiles, slabs, cells, width, cross, levels.shape[0])
        return per_device(plan, density, momentum, magnetic, energy, shifts, levels)

    return jax.shard_map(
        body,
        mesh=mesh,
        in_specs=(
            P("depth", "tile", None),
            P(None, "depth", "tile", None),
            P(None, "depth", "tile", None),
            P("depth", "tile", None),
            P(),
            P(),
        ),
        out_specs=(P(None, "depth", "tile", None), P(None, "tile", "depth")),
        check_vma=False,
    )
```

time: 83.8 us -> 38.5 us (0.46)
  the two profiles are of different devices: /device:TPU:27 before, /device:TPU:0 now
where the time goes in v1:
time: 38.5 us; the launch traced here: 38.3 us
  Pallas kernels  35.8 us (93%)
  local copies, waits for them, and re-layouts  1.89 us (5%)
  between operations  0.65 us (2%)
    pallas_call x1, Pallas kernels, per_device(): pl.pallas_call(functools.partial(section_kernel, plan), out_shape=(state_...  31.5 us
    pallas_call x1, Pallas kernels, per_device(): pl.pallas_call(functools.partial(ray_kernel, plan), out_shape=(state_shap...  4.27 us
    pallas_call x1, local copies, waits for them, and re-layouts, per_device(): pl.pallas_call(functools.partial(ray_kernel, plan), out_shape=(state_shap...  1.89 us

profile of v1, /device:TPU:0, one launch (start us, length us, event | category | flops | bytes accessed | tf_op | source)
XLA Modules:
  0.0 38.3 jit_solution(13519474731433639181)
XLA Ops:
  0.6 31.5 %section.1 = (f32[8,16,16,128]{3,2,1,0:T(8,128)}, f32[4,6,32,128]{3,2,1,0:T(8,128)}) custom-call(s32[24]{0:T(128)} %levels.3, f32[16,16,128]{2,1,0:T(8,128)} %density.1, f32[3,16,16,128]{3,2,1,0:T(8,128)} %momentum.1, f32[3,16,16,128]{3,2,1,0:T(8,128)} %magnetic.1, f32[16,16,128]{2,1,0:T(8,128)} %energy.1), custom_call_target="tpu_custom_call" | custom-call | tf_op jit(solution)/shard_map/section/pallas_call | solution.py:448
  32.1 4.3 %ray.1 = (f32[8,16,16,128]{3,2,1,0:T(8,128)}, f32[48,16,32]{2,1,0:T(8,128)}) custom-call(s32[24]{0:T(128)} %levels.3, s32[24]{0:T(128)} %shifts.1, f32[4,6,32,128]{3,2,1,0:T(8,128)} %get-tuple-element.4.lines, f32[8,16,16,128]{3,2,1,0:T(8,128)} %get-tuple-element.5.state_in), custom_call_target="tpu_custom_call" | custom-call | tf_op jit(solution)/shard_map/ray/pallas_call | solution.py:473
  36.4 1.9 %copy.8 = f32[48,16,32]{0,2,1:T(8,128)} copy(f32[48,16,32]{2,1,0:T(8,128)} %get-tuple-element.7) | data formatting | bytes 196608 | tf_op jit(solution)/shard_map/ray/pallas_call | solution.py:473

commit v2 on v1

v2 whole, which is shorter than its diff:
```python
import functools
import math

import jax
import jax.numpy as jnp
from jax import lax
from jax.experimental import pallas as pl
from jax.experimental.pallas import tpu as pltpu
from jax.sharding import PartitionSpec as P

W = 48
MOST = 8
GAMMA = 5.0 / 3.0
SECTION = 0.02
GRAVITY = 0.5
SIN_VIEW = 0.8660254037844386
COS_VIEW = 0.5
STRENGTH = 4.0
SPACING = 0.25
LOG2E = 1.4426950408889634
ROOT_LOG2E = math.sqrt(LOG2E)
F32 = jnp.float32
MESH = pl.DeviceIdType.MESH
PAD = 8


def column_shift(level):
    return (1732 * level + 1000) // 2000


def softplus(a):
    return jnp.maximum(a, 0.0) + jnp.log1p(jnp.exp(-jnp.abs(a)))


class Plan:
    def __init__(self, tiles, slabs, depth_cells, width, cross, positions, parts):
        self.tiles, self.slabs = tiles, slabs
        self.depth_cells, self.width, self.cross = depth_cells, width, cross
        self.positions = positions
        self.most = min(MOST, depth_cells)
        self.lanes = cross // slabs
        self.blocks = 128 // self.lanes
        self.items = 3 * self.most
        self.packed = -(-self.items // self.blocks)
        self.low = [column_shift(d * depth_cells) for d in range(slabs)]
        high = [column_shift((d + 1) * depth_cells - 1) for d in range(slabs)]
        self.rows = -(-(max(h - l for l, h in zip(self.low, high)) + width) // 8) * 8
        parts = min(parts, self.packed)
        cuts = [self.packed * i // parts for i in range(parts + 1)]
        self.pieces = []
        for d in range(slabs):
            mine = []
            for start, stop in zip(cuts[:-1], cuts[1:]):
                slot_low = start * self.blocks // 3
                slot_high = min(self.most - 1, (stop * self.blocks - 1) // 3)
                low = column_shift(d * depth_cells + slot_low)
                high = column_shift(d * depth_cells + depth_cells - self.most + slot_high)
                for o in range(low // width, (high + width - 1) // width + 1):
                    first = max(0, low - width * o)
                    last = min(width, high + width - width * o)
                    if last > first:
                        at = width * o + first - self.low[d]
                        mine.append((o, start, stop - start, first, last - first, at))
            self.pieces.append(mine)
        self.count = max(len(p) for p in self.pieces)
        self.reach = sorted({p[0] for mine in self.pieces for p in mine if p[0] % tiles})


def slab_start(levels, lowest, positions):
    ahead = jnp.int32(0)
    for k in range(positions):
        ahead = ahead + jnp.where(levels[k] < lowest, 1, 0)
    return ahead


def level_order(plan, levels, d, order):
    cells, most, positions = plan.depth_cells, plan.most, plan.positions
    lowest = d * cells
    ahead = slab_start(levels, lowest, positions)
    held = slab_start(levels, lowest + cells, positions) - ahead
    spare = most - held
    used = [
        jnp.where(
            i < held, levels[jnp.minimum(ahead + i, positions - 1)] - lowest, 2 * cells
        )
        for i in range(most)
    ]

    def free(rank):
        level = rank
        for one in used:
            level = level + jnp.where(one <= level, 1, 0)
        return level

    full = jnp.where(spare > 0, free(spare - 1) + 1, 0)
    for j in range(most):
        later = levels[jnp.clip(ahead + j - spare, 0, positions - 1)] - lowest
        order[j] = jnp.clip(jnp.where(j < full, j, later), 0, cells - 1)
    for j in range(cells - most):
        order[most + j] = jnp.clip(free(spare + j), 0, cells - 1)


def primitives(st, level):
    rho = st[0, level]
    mx, my, mz = st[1, level], st[2, level], st[3, level]
    bx, by, bz = st[4, level], st[5, level], st[6, level]
    en = st[7, level]
    inv = 1.0 / rho
    vx, vy, vz = mx * inv, my * inv, mz * inv
    half_sq = 0.5 * (bx * bx + by * by + bz * bz)
    kinetic = 0.5 * (mx * vx + my * vy + mz * vz)
    total = (GAMMA - 1.0) * (en - kinetic - half_sq) + half_sq
    vb = vx * bx + vy * by + vz * bz
    return rho, (mx, my, mz), (bx, by, bz), (vx, vy, vz), en, total, vb


def flux_along(axis, values):
    rho, m, b, v, en, total, vb = values
    out = [m[axis]]
    for i in range(3):
        term = m[i] * v[axis] - b[i] * b[axis]
        out.append(term + total if i == axis else term)
    for i in range(3):
        if i != axis:
            out.append(v[axis] * b[i] - b[axis] * v[i])
    out.append((en + total) * v[axis] - b[axis] * vb)
    return out


ROWS = ((0, 1, 2, 3, 5, 6, 7), (0, 1, 2, 3, 4, 6, 7), (0, 1, 2, 3, 4, 5, 7))
SCALE = SECTION / 60.0


def stencil(f):
    return SCALE * (45.0 * (f[4] - f[2]) - 9.0 * (f[5] - f[1]) + (f[6] - f[0]))


def section_kernel(
    plan, levels, density, momentum, magnetic, energy, state_out, lines_out,
    order, st, xf, zf, part, ns, pack, held, recv,
    in_sem, xs_sem, xr_sem, zs_sem, zr_sem, ds_sem, dr_sem, ls_sem, lr_sem, out_sem,
):
    tiles, slabs, cells, width = plan.tiles, plan.slabs, plan.depth_cells, plan.width
    most = plan.most
    t = lax.axis_index("tile")
    d = lax.axis_index("depth")
    right = lax.rem(t + 1, tiles)
    left = lax.rem(t + tiles - 1, tiles)

    loads = [
        pltpu.make_async_copy(density, st.at[0], in_sem.at[0]),
        pltpu.make_async_copy(momentum, st.at[1:4], in_sem.at[1]),
        pltpu.make_async_copy(magnetic, st.at[4:7], in_sem.at[2]),
        pltpu.make_async_copy(energy, st.at[7], in_sem.at[3]),
    ]
    for load in loads:
        load.start()

    barrier = pltpu.get_barrier_semaphore()

    def greet(tile, depth):
        pl.semaphore_signal(barrier, inc=1, device_id=(tile, depth), device_id_type=MESH)

    greet(right, d)
    greet(left, d)
    for i in range(1, slabs):
        greet(t, lax.rem(d + i, slabs))
    for o in plan.reach:
        greet(lax.rem(t + o, tiles), d)

    level_order(plan, levels, d, order)
    for load in loads:
        load.wait()

    def along_x(slot, carry):
        values = flux_along(0, primitives(st, order[slot]))
        for c in range(7):
            xf[c, slot, PAD:PAD + width, :] = values[c]
        return carry

    def x_copy(side, half):
        src = PAD + width - 3 if side == 0 else PAD
        dst = PAD - 3 if side == 0 else PAD + width
        slots = pl.ds(0, most) if half == 0 else pl.ds(most, cells - most)
        return pltpu.make_async_remote_copy(
            src_ref=xf.at[:, slots, pl.ds(src, 3), :],
            dst_ref=xf.at[:, slots, pl.ds(dst, 3), :],
            send_sem=xs_sem.at[side, half],
            recv_sem=xr_sem.at[side, half],
            device_id=(right if side == 0 else left, d),
            device_id_type=MESH,
        )

    def z_copy(side):
        src = cells if side == 0 else 3
        dst = 0 if side == 0 else cells + 3
        return pltpu.make_async_remote_copy(
            src_ref=zf.at[:, pl.ds(src, 3)],
            dst_ref=zf.at[:, pl.ds(dst, 3)],
            send_sem=zs_sem.at[side],
            recv_sem=zr_sem.at[side],
            device_id=(t, d + 1 if side == 0 else d - 1),
            device_id_type=MESH,
        )

    lax.fori_loop(0, most, along_x, 0)
    pl.semaphore_wait(barrier, 2 + (slabs - 1) + len(plan.reach))
    x_copy(0, 0).start()
    x_copy(1, 0).start()

    def along_z(level):
        values = flux_along(2, primitives(st, level))
        for c in range(7):
            zf[c, level + 3] = values[c]

    def rim(i, carry):
        along_z(i)
        along_z(cells - 3 + i)
        return carry

    lax.fori_loop(0, 3, rim, 0)

    @pl.when(d < slabs - 1)
    def _():
        z_copy(0).start()

    @pl.when(d > 0)
    def _():
        z_copy(1).start()

    halves = 2 if cells > most else 1
    if halves == 2:
        lax.fori_loop(most, cells, along_x, 0)
        x_copy(0, 1).start()
        x_copy(1, 1).start()

    def inner(level, carry):
        along_z(level)
        return carry

    lax.fori_loop(3, cells - 3, inner, 0)

    def cross(f):
        def at(step):
            return pltpu.roll(f, (-step) % plan.cross, 1)

        return stencil([at(i - 3) if i != 3 else f for i in range(7)])

    def along_y(level, carry):
        values = primitives(st, level)
        rho, m, b, _, en, _, _ = values
        base = [
            rho, m[0], m[1], m[2] + (SECTION * GRAVITY) * rho, b[0], b[1], b[2],
            en + (SECTION * GRAVITY) * m[2],
        ]
        flux = flux_along(1, values)
        for c, row in enumerate(ROWS[1]):
            base[row] = base[row] - cross(flux[c])
        for row in range(8):
            part[row, level] = base[row]
        return carry

    lax.fori_loop(0, cells, along_y, 0)

    @pl.when(d == 0)
    def _():
        for c in range(7):
            edge = zf[c, 3]
            for i in range(3):
                zf[c, i] = edge

    @pl.when(d > 0)
    def _():
        z_copy(0).wait_recv()

    @pl.when(d == slabs - 1)
    def _():
        for c in range(7):
            edge = zf[c, cells + 2]
            for i in range(3):
                zf[c, cells + 3 + i] = edge

    @pl.when(d < slabs - 1)
    def _():
        z_copy(1).wait_recv()

    def depth_part(level, carry):
        for c, row in enumerate(ROWS[2]):
            part[row, level] = part[row, level] - stencil([zf[c, level + i] for i in range(7)])
        return carry

    lax.fori_loop(0, cells, depth_part, 0)

    def finish(slot):
        level = order[slot]
        row_of = {row: c for c, row in enumerate(ROWS[0])}
        out = []
        for row in range(8):
            value = part[row, level]
            if row in row_of:
                c = row_of[row]
                value = value - stencil(
                    [xf[c, slot, pl.ds(PAD - 3 + i, width), :] for i in range(7)]
                )
            ns[row, slot] = value
            out.append(value)
        return out

    x_copy(0, 0).wait_recv()
    x_copy(1, 0).wait_recv()

    block_of = lax.broadcasted_iota(jnp.int32, (width, 128), 1) // plan.lanes
    rows = {}
    for slot in range(most):
        new = finish(slot)
        dens = 0.5 + softplus(new[0])
        inv = 1.0 / dens
        speed = (COS_VIEW * new[3] + SIN_VIEW * new[1]) * inv
        bx, by, bz = new[4], new[5], new[6]
        source = softplus(new[7] - 0.5 * (bx * bx + by * by + bz * bz)) * inv
        for f, value in enumerate((dens, speed, source)):
            item = 3 * slot + f
            row, block = item // plan.blocks, item % plan.blocks
            for target in range(slabs):
                shift = ((block - target) * plan.lanes) % 128
                moved = pltpu.roll(value, shift, 1) if shift else value
                earlier = rows.get((target, row))
                rows[target, row] = (
                    moved if earlier is None else jnp.where(block_of == block, moved, earlier)
                )
                if block == plan.blocks - 1 or item == plan.items - 1:
                    pack[target, row] = rows.pop((target, row))

    def depth_copy(step):
        target = lax.rem(d + step, slabs)
        return pltpu.make_async_remote_copy(
            src_ref=pack.at[target],
            dst_ref=held.at[d],
            send_sem=ds_sem.at[step],
            recv_sem=dr_sem.at[step],
            device_id=(t, target),
            device_id_type=MESH,
        )

    own = pltpu.make_async_copy(pack.at[d], held.at[d], dr_sem.at[0])
    own.start()
    for step in range(1, slabs):
        depth_copy(step).start()

    def line_copy(source, n):
        o, row, count, first, size, at = plan.pieces[source][n]
        src = held.at[source, pl.ds(row, count), pl.ds(first, size), :]
        dst = recv.at[source, pl.ds(row, count), pl.ds(at, size), :]
        if o % tiles == 0:
            return pltpu.make_async_copy(src, dst, lr_sem.at[source, n]), False
        return pltpu.make_async_remote_copy(
            src_ref=src,
            dst_ref=dst,
            send_sem=ls_sem.at[source, n],
            recv_sem=lr_sem.at[source, n],
            device_id=(lax.rem(t + tiles - o % tiles, tiles), d),
            device_id_type=MESH,
        ), True

    def forward(slab):
        for source in range(slabs):

            @pl.when(slab == source)
            def _():
                for n in range(len(plan.pieces[source])):
                    line_copy(source, n)[0].start()

    own.wait()
    forward(d)
    for step in range(1, slabs):
        depth_copy(step).wait_recv()
        forward(lax.rem(d + slabs - step, slabs))

    if halves == 2:
        x_copy(0, 1).wait_recv()
        x_copy(1, 1).wait_recv()

        def rest(slot, carry):
            finish(slot)
            return carry

        lax.fori_loop(most, cells, rest, 0)

    out_copy = pltpu.make_async_copy(ns, state_out, out_sem.at[0])
    out_copy.start()

    for source in range(slabs):
        for n in range(len(plan.pieces[source])):
            copy, remote = line_copy(source, n)
            if remote:
                copy.wait_recv()
            else:
                copy.wait()

    lines_copy = pltpu.make_async_copy(recv, lines_out, out_sem.at[1])
    lines_copy.start()

    for half in range(halves):
        x_copy(0, half).wait_send()
        x_copy(1, half).wait_send()

    @pl.when(d < slabs - 1)
    def _():
        z_copy(0).wait_send()

    @pl.when(d > 0)
    def _():
        z_copy(1).wait_send()

    for step in range(1, slabs):
        depth_copy(step).wait_send()
    for source in range(slabs):
        for n in range(len(plan.pieces[source])):
            copy, remote = line_copy(source, n)
            if remote:
                copy.wait_send()

    out_copy.wait()
    lines_copy.wait()


def ray_kernel(
    plan, levels, shifts, lines, state_in, state_out, intensity,
    order, rows, fields, hold, in_sem, state_sem, out_sem,
):
    slabs, cells, width, blocks = plan.slabs, plan.depth_cells, plan.width, plan.blocks
    lanes, positions, most = plan.lanes, plan.positions, plan.most
    lines_copy = pltpu.make_async_copy(lines, rows, in_sem)
    lines_copy.start()
    state_copy = pltpu.make_async_copy(state_in, hold, state_sem)
    state_copy.start()
    d = lax.axis_index("depth")
    level_order(plan, levels, d, order)

    slab = [levels[k] // cells for k in range(positions)]
    before = [jnp.int32(0)]
    for k in range(1, positions):
        before.append(jnp.where(slab[k] == slab[k - 1], before[-1] + 1, 0))
    held = [before[-1] + 1]
    for k in range(positions - 2, -1, -1):
        held.insert(0, jnp.where(slab[k] == slab[k + 1], held[0], before[k] + 1))
    slot = [
        before[k]
        + jnp.minimum(most - held[k], levels[k] - slab[k] * cells - before[k])
        for k in range(positions)
    ]

    lane = lax.broadcasted_iota(jnp.int32, (width, 128), 1)
    within = lax.rem(lane, lanes)
    wanted = lane // lanes == lax.rem(
        lax.broadcasted_iota(jnp.int32, (width, 128), 0), blocks
    )
    lines_copy.wait()
    for k in range(positions):
        start = shifts[k] - (1732 * (slab[k] * cells) + 1000) // 2000
        for f in range(3):
            item = 3 * slot[k] + f
            row, block = item // blocks, lax.rem(item, blocks)
            value = rows[slab[k], row, pl.ds(start, width), :]
            value = jnp.take_along_axis(value, within + block * lanes, axis=1)
            value = jnp.where(wanted, value, 0.0)
            step = 1
            while step < blocks:
                value = value + pltpu.roll(value, width - step, 0)
                step *= 2
            if f == 0:
                value = value * (-LOG2E * 2.0 / positions)
            elif f == 1:
                value = value * ROOT_LOG2E
            fields[f, k] = value

    state_copy.wait()
    out_copies = [
        pltpu.make_async_copy(hold.at[:, j], state_out.at[:, order[j]], out_sem.at[j])
        for j in range(cells)
    ]
    for copy in out_copies:
        copy.start()

    groups = W // 8
    for part in range(width // blocks):
        waves = [
            (
                (8 * g + lax.broadcasted_iota(jnp.int32, (8, 128), 0)).astype(F32)
                - 0.5 * (W - 1)
            )
            * (SPACING * ROOT_LOG2E)
            for g in range(groups)
        ]

        def field(f, k):
            return jnp.broadcast_to(fields[f, k, part * blocks:part * blocks + 1, :], (8, 128))

        def step(k, carry):
            seen, total = carry
            thin, speed, source = field(0, k), field(1, k), field(2, k)
            strong = STRENGTH * thin
            seen_next, total_next = [], []
            for g in range(groups):
                gap = waves[g] - speed
                depth = thin + strong * jnp.exp2(-(gap * gap))
                after = seen[g] * jnp.exp2(depth)
                total_next.append(total[g] + source * (seen[g] - after))
                seen_next.append(after)
            return tuple(seen_next), tuple(total_next)

        ones = tuple(jnp.ones((8, 128), F32) for _ in range(groups))
        zeros = tuple(jnp.zeros((8, 128), F32) for _ in range(groups))
        seen, total = lax.fori_loop(0, positions, step, (ones, zeros), unroll=4)
        last = field(2, positions - 1)
        value = jnp.concatenate([total[g] + last * seen[g] for g in range(groups)], axis=0)
        intensity[part * 128:(part + 1) * 128, :] = value.T

    for copy in out_copies:
        copy.wait()


def per_device(plan, density, momentum, magnetic, energy, shifts, levels):
    cells, width, cross = density.shape
    slabs = plan.slabs
    any_spec = pl.BlockSpec(memory_space=pl.ANY)
    scalars = pl.BlockSpec(memory_space=pltpu.SMEM)
    state_shape = jax.ShapeDtypeStruct((8, cells, width, cross), F32)
    lines_shape = jax.ShapeDtypeStruct((slabs, plan.packed, plan.rows, 128), F32)
    state, lines = pl.pallas_call(
        functools.partial(section_kernel, plan),
        out_shape=(state_shape, lines_shape),
        in_specs=[scalars] + [any_spec] * 4,
        out_specs=(any_spec, any_spec),
        scratch_shapes=[
            pltpu.SMEM((cells,), jnp.int32),
            pltpu.VMEM((8, cells, width, cross), F32),
            pltpu.VMEM((7, cells, width + 2 * PAD, cross), F32),
            pltpu.VMEM((7, cells + 6, width, cross), F32),
            pltpu.VMEM((8, cells, width, cross), F32),
            pltpu.VMEM((8, cells, width, cross), F32),
            pltpu.VMEM((slabs, plan.packed, width, 128), F32),
            pltpu.VMEM((slabs, plan.packed, width, 128), F32),
            pltpu.VMEM((slabs, plan.packed, plan.rows, 128), F32),
            pltpu.SemaphoreType.DMA((4,)),
            pltpu.SemaphoreType.DMA((2, 2)),
            pltpu.SemaphoreType.DMA((2, 2)),
            pltpu.SemaphoreType.DMA((2,)),
            pltpu.SemaphoreType.DMA((2,)),
            pltpu.SemaphoreType.DMA((slabs,)),
            pltpu.SemaphoreType.DMA((slabs,)),
            pltpu.SemaphoreType.DMA((slabs, plan.count)),
            pltpu.SemaphoreType.DMA((slabs, plan.count)),
            pltpu.SemaphoreType.DMA((2,)),
        ],
        compiler_params=pltpu.CompilerParams(collective_id=0, has_side_effects=True),
        name="section",
    )(levels, density, momentum, magnetic, energy)
    new_state, intensity = pl.pallas_call(
        functools.partial(ray_kernel, plan),
        out_shape=(state_shape, jax.ShapeDtypeStruct((width * plan.lanes, W), F32)),
        in_specs=[scalars, scalars, any_spec, any_spec],
        out_specs=(any_spec, pl.BlockSpec(memory_space=pltpu.VMEM)),
        scratch_shapes=[
            pltpu.SMEM((cells,), jnp.int32),
            pltpu.VMEM((slabs, plan.packed, plan.rows, 128), F32),
            pltpu.VMEM((3, plan.positions, width, 128), F32),
            pltpu.VMEM((8, cells, width, cross), F32),
            pltpu.SemaphoreType.DMA,
            pltpu.SemaphoreType.DMA,
            pltpu.SemaphoreType.DMA((cells,)),
        ],
        name="ray",
    )(levels, shifts, lines, state)
    intensity = intensity.reshape(width, plan.lanes, W)
    return new_state, jnp.transpose(intensity, (2, 0, 1))


def solution(mesh):
    tiles, slabs = mesh.shape["tile"], mesh.shape["depth"]

    def body(density, momentum, magnetic, energy, shifts, levels):
        cells, width, cross = density.shape
        plan = Plan(tiles, slabs, cells, width, cross, levels.shape[0], 2)
        return per_device(plan, density, momentum, magnetic, energy, shifts, levels)

    return jax.shard_map(
        body,
        mesh=mesh,
        in_specs=(
            P("depth", "tile", None),
            P(None, "depth", "tile", None),
            P(None, "depth", "tile", None),
            P("depth", "tile", None),
            P(),
            P(),
        ),
        out_specs=(P(None, "depth", "tile", None), P(None, "tile", "depth")),
        check_vma=False,
    )
```

time: 38.5 us -> 29.6 us (0.77)
  Pallas kernels: 35.8 us -> 28.8 us
  local copies, waits for them, and re-layouts: 1.89 us -> 0 us
    pallas_call x1, Pallas kernels: 31.5 us -> 24.1 us  [per_device(): pl.pallas_call(functools.partial(section_kernel, plan), out_shape=(state_...]
    pallas_call x1 -> x0, local copies, waits for them, and re-layouts: 1.89 us -> none  [per_device(): pl.pallas_call(functools.partial(ray_kernel, plan), out_shape=(state_shap...]
    pallas_call x1, Pallas kernels: 4.27 us -> 4.67 us  [per_device(): pl.pallas_call(functools.partial(ray_kernel, plan), out_shape=(state_shap...]
where the time goes in v2:
time: 29.6 us; the launch traced here: 29.4 us
  Pallas kernels  28.8 us (97%)
  between operations  0.64 us (2%)
    pallas_call x1, Pallas kernels, per_device(): pl.pallas_call(functools.partial(section_kernel, plan), out_shape=(state_...  24.1 us
    pallas_call x1, Pallas kernels, per_device(): pl.pallas_call(functools.partial(ray_kernel, plan), out_shape=(state_shap...  4.67 us

profile of v2, /device:TPU:0, one launch (start us, length us, event | category | flops | bytes accessed | tf_op | source)
XLA Modules:
  0.0 29.4 jit_solution(13290345092467402868)
XLA Ops:
  0.6 24.1 %section.1 = (f32[8,16,16,128]{3,2,1,0:T(8,128)}, f32[4,6,32,128]{3,2,1,0:T(8,128)}) custom-call(s32[24]{0:T(128)} %levels.3, f32[16,16,128]{2,1,0:T(8,128)} %density.1, f32[3,16,16,128]{3,2,1,0:T(8,128)} %momentum.1, f32[3,16,16,128]{3,2,1,0:T(8,128)} %magnetic.1, f32[16,16,128]{2,1,0:T(8,128)} %energy.1), custom_call_target="tpu_custom_call" | custom-call | tf_op jit(solution)/shard_map/section/pallas_call | solution.py:530
  24.8 4.7 %ray.1 = (f32[8,16,16,128]{3,2,1,0:T(8,128)}, f32[512,48]{1,0:T(8,128)}) custom-call(s32[24]{0:T(128)} %levels.3, s32[24]{0:T(128)} %shifts.1, f32[4,6,32,128]{3,2,1,0:T(8,128)} %get-tuple-element.6.lines, f32[8,16,16,128]{3,2,1,0:T(8,128)} %get-tuple-element.7.state_in), custom_call_target="tpu_custom_call" | custom-call | tf_op jit(solution)/shard_map/ray/pallas_call | solution.py:559

commit v3 on v2

--- a/solution.py
+++ b/solution.py
@@ -47,10 +47,16 @@
         self.rows = -(-(max(h - l for l, h in zip(self.low, high)) + width) // 8) * 8
         parts = min(parts, self.packed)
         cuts = [self.packed * i // parts for i in range(parts + 1)]
+        self.groups = list(zip(cuts[:-1], cuts[1:]))
+        ends = [min(self.most, -(-stop * self.blocks // 3)) for _, stop in self.groups]
+        ends.append(depth_cells)
+        self.spans = list(zip([0] + ends[:-1], ends))
+        if self.spans[-1][0] == self.spans[-1][1]:
+            self.spans.pop()
         self.pieces = []
         for d in range(slabs):
             mine = []
-            for start, stop in zip(cuts[:-1], cuts[1:]):
+            for group, (start, stop) in enumerate(self.groups):
                 slot_low = start * self.blocks // 3
                 slot_high = min(self.most - 1, (stop * self.blocks - 1) // 3)
                 low = column_shift(d * depth_cells + slot_low)
@@ -60,7 +66,7 @@
                     last = min(width, high + width - width * o)
                     if last > first:
                         at = width * o + first - self.low[d]
-                        mine.append((o, start, stop - start, first, last - first, at))
+                        mine.append((o, group, first, last - first, at))
             self.pieces.append(mine)
         self.count = max(len(p) for p in self.pieces)
         self.reach = sorted({p[0] for mine in self.pieces for p in mine if p[0] % tiles})
@@ -100,6 +106,23 @@
         order[most + j] = jnp.clip(free(spare + j), 0, cells - 1)
 
 
+def ray_order(plan, levels, shifts, order):
+    cells, most, positions = plan.depth_cells, plan.most, plan.positions
+    slab = [levels[k] // cells for k in range(positions)]
+    before = [jnp.int32(0)]
+    for k in range(1, positions):
+        before.append(jnp.where(slab[k] == slab[k - 1], before[-1] + 1, 0))
+    held = [before[-1] + 1]
+    for k in range(positions - 2, -1, -1):
+        held.insert(0, jnp.where(slab[k] == slab[k + 1], held[0], before[k] + 1))
+    for k in range(positions):
+        spare = jnp.minimum(most - held[k], levels[k] - slab[k] * cells - before[k])
+        at = cells + 3 * k
+        order[at] = slab[k]
+        order[at + 1] = before[k] + spare
+        order[at + 2] = shifts[k] - (1732 * (slab[k] * cells) + 1000) // 2000
+
+
 def primitives(st, level):
     rho = st[0, level]
     mx, my, mz = st[1, level], st[2, level], st[3, level]
@@ -136,9 +159,9 @@
 
 
 def section_kernel(
-    plan, levels, density, momentum, magnetic, energy, state_out, lines_out,
-    order, st, xf, zf, part, ns, pack, held, recv,
-    in_sem, xs_sem, xr_sem, zs_sem, zr_sem, ds_sem, dr_sem, ls_sem, lr_sem, out_sem,
+    plan, levels_in, shifts_in, density, momentum, magnetic, energy, ns, recv, order,
+    levels, shifts, st, xf, zf, part, pack, held,
+    in_sem, xs_sem, xr_sem, zs_sem, zr_sem, ds_sem, dr_sem, ls_sem, lr_sem,
 ):
     tiles, slabs, cells, width = plan.tiles, plan.slabs, plan.depth_cells, plan.width
     most = plan.most
@@ -153,7 +176,11 @@
         pltpu.make_async_copy(magnetic, st.at[4:7], in_sem.at[2]),
         pltpu.make_async_copy(energy, st.at[7], in_sem.at[3]),
     ]
-    for load in loads:
+    index_loads = [
+        pltpu.make_async_copy(levels_in, levels, in_sem.at[4]),
+        pltpu.make_async_copy(shifts_in, shifts, in_sem.at[5]),
+    ]
+    for load in index_loads + loads:
         load.start()
 
     barrier = pltpu.get_barrier_semaphore()
@@ -168,6 +195,8 @@
     for o in plan.reach:
         greet(lax.rem(t + o, tiles), d)
 
+    for load in index_loads:
+        load.wait()
     level_order(plan, levels, d, order)
     for load in loads:
         load.wait()
@@ -178,15 +207,16 @@
             xf[c, slot, PAD:PAD + width, :] = values[c]
         return carry
 
-    def x_copy(side, half):
+    def x_copy(side, span):
         src = PAD + width - 3 if side == 0 else PAD
         dst = PAD - 3 if side == 0 else PAD + width
-        slots = pl.ds(0, most) if half == 0 else pl.ds(most, cells - most)
+        start, stop = plan.spans[span]
+        slots = pl.ds(start, stop - start)
         return pltpu.make_async_remote_copy(
             src_ref=xf.at[:, slots, pl.ds(src, 3), :],
             dst_ref=xf.at[:, slots, pl.ds(dst, 3), :],
-            send_sem=xs_sem.at[side, half],
-            recv_sem=xr_sem.at[side, half],
+            send_sem=xs_sem.at[side, span],
+            recv_sem=xr_sem.at[side, span],
             device_id=(right if side == 0 else left, d),
             device_id_type=MESH,
         )
@@ -203,10 +233,15 @@
             device_id_type=MESH,
         )
 
-    lax.fori_loop(0, most, along_x, 0)
+    spans, groups = len(plan.spans), len(plan.groups)
+    lax.fori_loop(0, plan.spans[0][1], along_x, 0)
     pl.semaphore_wait(barrier, 2 + (slabs - 1) + len(plan.reach))
     x_copy(0, 0).start()
     x_copy(1, 0).start()
+    for span in range(1, groups):
+        lax.fori_loop(plan.spans[span][0], plan.spans[span][1], along_x, 0)
+        x_copy(0, span).start()
+        x_copy(1, span).start()
 
     def along_z(level):
         values = flux_along(2, primitives(st, level))
@@ -228,11 +263,10 @@
     def _():
         z_copy(1).start()
 
-    halves = 2 if cells > most else 1
-    if halves == 2:
-        lax.fori_loop(most, cells, along_x, 0)
-        x_copy(0, 1).start()
-        x_copy(1, 1).start()
+    for span in range(groups, spans):
+        lax.fori_loop(plan.spans[span][0], plan.spans[span][1], along_x, 0)
+        x_copy(0, span).start()
+        x_copy(1, span).start()
 
     def inner(level, carry):
         along_z(level)
@@ -290,6 +324,7 @@
         return carry
 
     lax.fori_loop(0, cells, depth_part, 0)
+    ray_order(plan, levels, shifts, order)
 
     def finish(slot):
         level = order[slot]
@@ -306,12 +341,10 @@
             out.append(value)
         return out
 
-    x_copy(0, 0).wait_recv()
-    x_copy(1, 0).wait_recv()
-
     block_of = lax.broadcasted_iota(jnp.int32, (width, 128), 1) // plan.lanes
     rows = {}
-    for slot in range(most):
+
+    def emit(slot):
         new = finish(slot)
         dens = 0.5 + softplus(new[0])
         inv = 1.0 / dens
@@ -331,26 +364,28 @@
                 if block == plan.blocks - 1 or item == plan.items - 1:
                     pack[target, row] = rows.pop((target, row))
 
-    def depth_copy(step):
+    def depth_copy(step, group):
         target = lax.rem(d + step, slabs)
+        start, stop = plan.groups[group]
+        part_rows = pl.ds(start, stop - start)
+        if step == 0:
+            return pltpu.make_async_copy(
+                pack.at[d, part_rows], held.at[d, part_rows], dr_sem.at[0, group]
+            )
         return pltpu.make_async_remote_copy(
-            src_ref=pack.at[target],
-            dst_ref=held.at[d],
-            send_sem=ds_sem.at[step],
-            recv_sem=dr_sem.at[step],
+            src_ref=pack.at[target, part_rows],
+            dst_ref=held.at[d, part_rows],
+            send_sem=ds_sem.at[step, group],
+            recv_sem=dr_sem.at[step, group],
             device_id=(t, target),
             device_id_type=MESH,
         )
 
-    own = pltpu.make_async_copy(pack.at[d], held.at[d], dr_sem.at[0])
-    own.start()
-    for step in range(1, slabs):
-        depth_copy(step).start()
-
     def line_copy(source, n):
-        o, row, count, first, size, at = plan.pieces[source][n]
-        src = held.at[source, pl.ds(row, count), pl.ds(first, size), :]
-        dst = recv.at[source, pl.ds(row, count), pl.ds(at, size), :]
+        o, group, first, size, at = plan.pieces[source][n]
+        start, stop = plan.groups[group]
+        src = held.at[source, pl.ds(start, stop - start), pl.ds(first, size), :]
+        dst = recv.at[source, pl.ds(start, stop - start), pl.ds(at, size), :]
         if o % tiles == 0:
             return pltpu.make_async_copy(src, dst, lr_sem.at[source, n]), False
         return pltpu.make_async_remote_copy(
@@ -362,32 +397,38 @@
             device_id_type=MESH,
         ), True
 
-    def forward(slab):
+    def forward(slab, group):
         for source in range(slabs):
 
             @pl.when(slab == source)
             def _():
-                for n in range(len(plan.pieces[source])):
-                    line_copy(source, n)[0].start()
-
-    own.wait()
-    forward(d)
-    for step in range(1, slabs):
-        depth_copy(step).wait_recv()
-        forward(lax.rem(d + slabs - step, slabs))
-
-    if halves == 2:
-        x_copy(0, 1).wait_recv()
-        x_copy(1, 1).wait_recv()
-
-        def rest(slot, carry):
-            finish(slot)
-            return carry
-
-        lax.fori_loop(most, cells, rest, 0)
-
-    out_copy = pltpu.make_async_copy(ns, state_out, out_sem.at[0])
-    out_copy.start()
+                for n, piece in enumerate(plan.pieces[source]):
+                    if piece[1] == group:
+                        line_copy(source, n)[0].start()
+
+    for group in range(groups):
+        x_copy(0, group).wait_recv()
+        x_copy(1, group).wait_recv()
+        for slot in range(*plan.spans[group]):
+            emit(slot)
+        for step in range(slabs):
+            depth_copy(step, group).start()
+        depth_copy(0, group).wait()
+        forward(d, group)
+
+    for group in range(groups):
+        for step in range(1, slabs):
+            depth_copy(step, group).wait_recv()
+            forward(lax.rem(d + slabs - step, slabs), group)
+
+    def rest(slot, carry):
+        finish(slot)
+        return carry
+
+    for span in range(groups, spans):
+        x_copy(0, span).wait_recv()
+        x_copy(1, span).wait_recv()
+        lax.fori_loop(plan.spans[span][0], plan.spans[span][1], rest, 0)
 
     for source in range(slabs):
         for n in range(len(plan.pieces[source])):
@@ -397,12 +438,9 @@
             else:
                 copy.wait()
 
-    lines_copy = pltpu.make_async_copy(recv, lines_out, out_sem.at[1])
-    lines_copy.start()
-
-    for half in range(halves):
-        x_copy(0, half).wait_send()
-        x_copy(1, half).wait_send()
+    for span in range(spans):
+        x_copy(0, span).wait_send()
+        x_copy(1, span).wait_send()
 
     @pl.when(d < slabs - 1)
     def _():
@@ -412,56 +450,38 @@
     def _():
         z_copy(1).wait_send()
 
-    for step in range(1, slabs):
-        depth_copy(step).wait_send()
+    for group in range(groups):
+        for step in range(1, slabs):
+            depth_copy(step, group).wait_send()
     for source in range(slabs):
         for n in range(len(plan.pieces[source])):
             copy, remote = line_copy(source, n)
             if remote:
                 copy.wait_send()
 
-    out_copy.wait()
-    lines_copy.wait()
-
-
-def ray_kernel(
-    plan, levels, shifts, lines, state_in, state_out, intensity,
-    order, rows, fields, hold, in_sem, state_sem, out_sem,
-):
-    slabs, cells, width, blocks = plan.slabs, plan.depth_cells, plan.width, plan.blocks
-    lanes, positions, most = plan.lanes, plan.positions, plan.most
-    lines_copy = pltpu.make_async_copy(lines, rows, in_sem)
-    lines_copy.start()
-    state_copy = pltpu.make_async_copy(state_in, hold, state_sem)
-    state_copy.start()
-    d = lax.axis_index("depth")
-    level_order(plan, levels, d, order)
-
-    slab = [levels[k] // cells for k in range(positions)]
-    before = [jnp.int32(0)]
-    for k in range(1, positions):
-        before.append(jnp.where(slab[k] == slab[k - 1], before[-1] + 1, 0))
-    held = [before[-1] + 1]
-    for k in range(positions - 2, -1, -1):
-        held.insert(0, jnp.where(slab[k] == slab[k + 1], held[0], before[k] + 1))
-    slot = [
-        before[k]
-        + jnp.minimum(most - held[k], levels[k] - slab[k] * cells - before[k])
-        for k in range(positions)
+
+def ray_kernel(plan, order, rows, hold, state_out, intensity, fields, out_sem):
+    cells, width, blocks = plan.depth_cells, plan.width, plan.blocks
+    lanes, positions = plan.lanes, plan.positions
+    out_copies = [
+        pltpu.make_async_copy(hold.at[:, j], state_out.at[:, order[j]], out_sem.at[j])
+        for j in range(cells)
     ]
+    for copy in out_copies:
+        copy.start()
 
     lane = lax.broadcasted_iota(jnp.int32, (width, 128), 1)
     within = lax.rem(lane, lanes)
     wanted = lane // lanes == lax.rem(
         lax.broadcasted_iota(jnp.int32, (width, 128), 0), blocks
     )
-    lines_copy.wait()
     for k in range(positions):
-        start = shifts[k] - (1732 * (slab[k] * cells) + 1000) // 2000
+        at = cells + 3 * k
+        slab, slot, start = order[at], order[at + 1], order[at + 2]
         for f in range(3):
-            item = 3 * slot[k] + f
+            item = 3 * slot + f
             row, block = item // blocks, lax.rem(item, blocks)
-            value = rows[slab[k], row, pl.ds(start, width), :]
+            value = rows[slab, row, pl.ds(start, width), :]
             value = jnp.take_along_axis(value, within + block * lanes, axis=1)
             value = jnp.where(wanted, value, 0.0)
             step = 1
@@ -473,14 +493,6 @@
             elif f == 1:
                 value = value * ROOT_LOG2E
             fields[f, k] = value
-
-    state_copy.wait()
-    out_copies = [
-        pltpu.make_async_copy(hold.at[:, j], state_out.at[:, order[j]], out_sem.at[j])
-        for j in range(cells)
-    ]
-    for copy in out_copies:
-        copy.start()
 
     groups = W // 8
     for part in range(width // blocks):
@@ -511,7 +523,7 @@
 
         ones = tuple(jnp.ones((8, 128), F32) for _ in range(groups))
         zeros = tuple(jnp.zeros((8, 128), F32) for _ in range(groups))
-        seen, total = lax.fori_loop(0, positions, step, (ones, zeros), unroll=4)
+        seen, total = lax.fori_loop(0, positions, step, (ones, zeros), unroll=8)
         last = field(2, positions - 1)
         value = jnp.concatenate([total[g] + last * seen[g] for g in range(groups)], axis=0)
         intensity[part * 128:(part + 1) * 128, :] = value.T
@@ -525,53 +537,63 @@
     slabs = plan.slabs
     any_spec = pl.BlockSpec(memory_space=pl.ANY)
     scalars = pl.BlockSpec(memory_space=pltpu.SMEM)
-    state_shape = jax.ShapeDtypeStruct((8, cells, width, cross), F32)
-    lines_shape = jax.ShapeDtypeStruct((slabs, plan.packed, plan.rows, 128), F32)
-    state, lines = pl.pallas_call(
+    vmem = pl.BlockSpec(memory_space=pltpu.VMEM)
+    state_shape = (8, cells, width, cross)
+    lines_shape = (slabs, plan.packed, plan.rows, 128)
+    parts, spans = len(plan.groups), len(plan.spans)
+    state, lines, order = pl.pallas_call(
         functools.partial(section_kernel, plan),
-        out_shape=(state_shape, lines_shape),
-        in_specs=[scalars] + [any_spec] * 4,
-        out_specs=(any_spec, any_spec),
+        out_shape=(
+            pltpu.VMEM(state_shape, F32),
+            pltpu.VMEM(lines_shape, F32),
+            jax.ShapeDtypeStruct((cells + 3 * plan.positions,), jnp.int32),
+        ),
+        in_specs=[pl.BlockSpec(memory_space=pltpu.HBM)] * 6,
+        out_specs=(vmem, vmem, scalars),
         scratch_shapes=[
-            pltpu.SMEM((cells,), jnp.int32),
-            pltpu.VMEM((8, cells, width, cross), F32),
+            pltpu.SMEM((plan.positions,), jnp.int32),
+            pltpu.SMEM((plan.positions,), jnp.int32),
+            pltpu.VMEM(state_shape, F32),
             pltpu.VMEM((7, cells, width + 2 * PAD, cross), F32),
             pltpu.VMEM((7, cells + 6, width, cross), F32),
-            pltpu.VMEM((8, cells, width, cross), F32),
-            pltpu.VMEM((8, cells, width, cross), F32),
+            pltpu.VMEM(state_shape, F32),
             pltpu.VMEM((slabs, plan.packed, width, 128), F32),
             pltpu.VMEM((slabs, plan.packed, width, 128), F32),
-            pltpu.VMEM((slabs, plan.packed, plan.rows, 128), F32),
-            pltpu.SemaphoreType.DMA((4,)),
-            pltpu.SemaphoreType.DMA((2, 2)),
-            pltpu.SemaphoreType.DMA((2, 2)),
+            pltpu.SemaphoreType.DMA((6,)),
+            pltpu.SemaphoreType.DMA((2, spans)),
+            pltpu.SemaphoreType.DMA((2, spans)),
             pltpu.SemaphoreType.DMA((2,)),
             pltpu.SemaphoreType.DMA((2,)),
-            pltpu.SemaphoreType.DMA((slabs,)),
-            pltpu.SemaphoreType.DMA((slabs,)),
+            pltpu.SemaphoreType.DMA((slabs, parts)),
+            pltpu.SemaphoreType.DMA((slabs, parts)),
             pltpu.SemaphoreType.DMA((slabs, plan.count)),
             pltpu.SemaphoreType.DMA((slabs, plan.count)),
-            pltpu.SemaphoreType.DMA((2,)),
         ],
-        compiler_params=pltpu.CompilerParams(collective_id=0, has_side_effects=True),
+        compiler_params=pltpu.CompilerParams(
+            collective_id=0, has_side_effects=True, vmem_limit_bytes=16 << 20
+        ),
         name="section",
-    )(levels, density, momentum, magnetic, energy)
+    )(*(
+        pltpu.with_memory_space_constraint(x, pltpu.HBM)
+        for x in (levels, shifts, density, momentum, magnetic, energy)
+    ))
+    lines = pltpu.with_memory_space_constraint(lines, pltpu.VMEM)
+    state = pltpu.with_memory_space_constraint(state, pltpu.VMEM)
     new_state, intensity = pl.pallas_call(
         functools.partial(ray_kernel, plan),
-        out_shape=(state_shape, jax.ShapeDtypeStruct((width * plan.lanes, W), F32)),
-        in_specs=[scalars, scalars, any_spec, any_spec],
-        out_specs=(any_spec, pl.BlockSpec(memory_space=pltpu.VMEM)),
+        out_shape=(
+            jax.ShapeDtypeStruct(state_shape, F32),
+            jax.ShapeDtypeStruct((width * plan.lanes, W), F32),
+        ),
+        in_specs=[scalars, vmem, vmem],
+        out_specs=(any_spec, vmem),
         scratch_shapes=[
-            pltpu.SMEM((cells,), jnp.int32),
-            pltpu.VMEM((slabs, plan.packed, plan.rows, 128), F32),
             pltpu.VMEM((3, plan.positions, width, 128), F32),
-            pltpu.VMEM((8, cells, width, cross), F32),
-            pltpu.SemaphoreType.DMA,
-            pltpu.SemaphoreType.DMA,
             pltpu.SemaphoreType.DMA((cells,)),
         ],
+        compiler_params=pltpu.CompilerParams(vmem_limit_bytes=16 << 20),
         name="ray",
-    )(levels, shifts, lines, state)
+    )(order, lines, state)
     intensity = intensity.reshape(width, plan.lanes, W)
     return new_state, jnp.transpose(intensity, (2, 0, 1))
 

time: 29.6 us -> 27.4 us (0.926)
  Pallas kernels: 28.8 us -> 26.6 us
    pallas_call x2, Pallas kernels: 28.8 us -> 26.6 us  [the longest x1 23.4 us: per_device(): pl.pallas_call(functools.partial(section_kernel, plan), out_shape=(pltpu....]
where the time goes in v3:
time: 27.4 us; the launch traced here: 27.3 us
  Pallas kernels  26.6 us (97%)
  between operations  0.64 us (2%)
    pallas_call x1, Pallas kernels, per_device(): pl.pallas_call(functools.partial(section_kernel, plan), out_shape=(pltpu....  23.4 us
    pallas_call x1, Pallas kernels, per_device(): pl.pallas_call(functools.partial(ray_kernel, plan), out_shape=(jax.ShapeD...  3.24 us

profile of v3, /device:TPU:0, one launch (start us, length us, event | category | flops | bytes accessed | tf_op | source)
XLA Modules:
  0.0 27.3 jit_solution(636209196979218652)
XLA Ops:
  0.6 23.4 %section.1 = (f32[8,16,16,128]{3,2,1,0:T(8,128)S(1)}, f32[4,6,32,128]{3,2,1,0:T(8,128)S(1)}, s32[88]{0:T(128)S(1)}) custom-call(s32[24]{0:T(128)} %levels_in.1, s32[24]{0:T(128)} %shifts_in.1, f32[16,16,128]{2,1,0:T(8,128)} %density.1, f32[3,16,16,128]{3,2,1,0:T(8,128)} %momentum.1, f32[3,16,16,128]{3,2,1,0:T(8,128)} %magnetic.1, f32[16,16,128]{2,1,0:T(8,128)} %energy.1), custom_call_target="tpu_custom_call" | custom-call | tf_op jit(solution)/shard_map/section/pallas_call | solution.py:544
  24.0 3.2 %ray.1 = (f32[8,16,16,128]{3,2,1,0:T(8,128)}, f32[512,48]{1,0:T(8,128)}) custom-call(s32[88]{0:T(128)S(1)} %get-tuple-element.7.order, f32[4,6,32,128]{3,2,1,0:T(8,128)S(1)} %get-tuple-element.8.rows, f32[8,16,16,128]{3,2,1,0:T(8,128)S(1)} %get-tuple-element.9.hold), custom_call_target="tpu_custom_call" | custom-call | tf_op jit(solution)/shard_map/ray/pallas_call | solution.py:582

commit v4 on v3

--- a/solution.py
+++ b/solution.py
@@ -48,11 +48,10 @@
         parts = min(parts, self.packed)
         cuts = [self.packed * i // parts for i in range(parts + 1)]
         self.groups = list(zip(cuts[:-1], cuts[1:]))
-        ends = [min(self.most, -(-stop * self.blocks // 3)) for _, stop in self.groups]
-        ends.append(depth_cells)
-        self.spans = list(zip([0] + ends[:-1], ends))
-        if self.spans[-1][0] == self.spans[-1][1]:
-            self.spans.pop()
+        self.spans = [(0, self.most)]
+        if depth_cells > self.most:
+            self.spans.append((self.most, depth_cells))
+        self.core = width - 6
         self.pieces = []
         for d in range(slabs):
             mine = []
@@ -62,11 +61,13 @@
                 low = column_shift(d * depth_cells + slot_low)
                 high = column_shift(d * depth_cells + depth_cells - self.most + slot_high)
                 for o in range(low // width, (high + width - 1) // width + 1):
-                    first = max(0, low - width * o)
-                    last = min(width, high + width - width * o)
-                    if last > first:
-                        at = width * o + first - self.low[d]
-                        mine.append((o, group, first, last - first, at))
+                    for kind, left, right in ((0, 3, width - 3), (1, 0, 3), (1, width - 3, width)):
+                        first = max(left, low - width * o)
+                        last = min(right, high + width - width * o)
+                        if last > first:
+                            at = width * o + first - self.low[d]
+                            row = first - (3 if kind == 0 else left and width - 8)
+                            mine.append((o, group, row, last - first, at, kind))
             self.pieces.append(mine)
         self.count = max(len(p) for p in self.pieces)
         self.reach = sorted({p[0] for mine in self.pieces for p in mine if p[0] % tiles})
@@ -160,7 +161,7 @@
 
 def section_kernel(
     plan, levels_in, shifts_in, density, momentum, magnetic, energy, ns, recv, order,
-    levels, shifts, st, xf, zf, part, pack, held,
+    levels, shifts, st, xf, zf, part, pack, rim_pack, held, rim_held,
     in_sem, xs_sem, xr_sem, zs_sem, zr_sem, ds_sem, dr_sem, ls_sem, lr_sem,
 ):
     tiles, slabs, cells, width = plan.tiles, plan.slabs, plan.depth_cells, plan.width
@@ -233,15 +234,7 @@
             device_id_type=MESH,
         )
 
-    spans, groups = len(plan.spans), len(plan.groups)
-    lax.fori_loop(0, plan.spans[0][1], along_x, 0)
-    pl.semaphore_wait(barrier, 2 + (slabs - 1) + len(plan.reach))
-    x_copy(0, 0).start()
-    x_copy(1, 0).start()
-    for span in range(1, groups):
-        lax.fori_loop(plan.spans[span][0], plan.spans[span][1], along_x, 0)
-        x_copy(0, span).start()
-        x_copy(1, span).start()
+    spans = len(plan.spans)
 
     def along_z(level):
         values = flux_along(2, primitives(st, level))
@@ -254,6 +247,8 @@
         return carry
 
     lax.fori_loop(0, 3, rim, 0)
+    lax.fori_loop(*plan.spans[0], along_x, 0)
+    pl.semaphore_wait(barrier, 2 + (slabs - 1) + len(plan.reach))
 
     @pl.when(d < slabs - 1)
     def _():
@@ -263,8 +258,10 @@
     def _():
         z_copy(1).start()
 
-    for span in range(groups, spans):
-        lax.fori_loop(plan.spans[span][0], plan.spans[span][1], along_x, 0)
+    x_copy(0, 0).start()
+    x_copy(1, 0).start()
+    for span in range(1, spans):
+        lax.fori_loop(*plan.spans[span], along_x, 0)
         x_copy(0, span).start()
         x_copy(1, span).start()
 
@@ -341,50 +338,54 @@
             out.append(value)
         return out
 
-    block_of = lax.broadcasted_iota(jnp.int32, (width, 128), 1) // plan.lanes
+    def emit(new, out, height):
+        block_of = lax.broadcasted_iota(jnp.int32, (height, 128), 1) // plan.lanes
+        for slot in range(most):
+            rho, mx, mz, bx, by, bz, en = new(slot)
+            dens = 0.5 + softplus(rho)
+            inv = 1.0 / dens
+            speed = (COS_VIEW * mz + SIN_VIEW * mx) * inv
+            source = softplus(en - 0.5 * (bx * bx + by * by + bz * bz)) * inv
+            for f, value in enumerate((dens, speed, source)):
+                item = 3 * slot + f
+                row, block = item // plan.blocks, item % plan.blocks
+                for target in range(slabs):
+                    shift = ((block - target) * plan.lanes) % 128
+                    moved = pltpu.roll(value, shift, 1) if shift else value
+                    if block:
+                        moved = jnp.where(block_of == block, moved, rows[target, row])
+                    rows[target, row] = moved
+                    if block == plan.blocks - 1 or item == plan.items - 1:
+                        out[target, row] = rows.pop((target, row))
+
     rows = {}
-
-    def emit(slot):
-        new = finish(slot)
-        dens = 0.5 + softplus(new[0])
-        inv = 1.0 / dens
-        speed = (COS_VIEW * new[3] + SIN_VIEW * new[1]) * inv
-        bx, by, bz = new[4], new[5], new[6]
-        source = softplus(new[7] - 0.5 * (bx * bx + by * by + bz * bz)) * inv
-        for f, value in enumerate((dens, speed, source)):
-            item = 3 * slot + f
-            row, block = item // plan.blocks, item % plan.blocks
-            for target in range(slabs):
-                shift = ((block - target) * plan.lanes) % 128
-                moved = pltpu.roll(value, shift, 1) if shift else value
-                earlier = rows.get((target, row))
-                rows[target, row] = (
-                    moved if earlier is None else jnp.where(block_of == block, moved, earlier)
-                )
-                if block == plan.blocks - 1 or item == plan.items - 1:
-                    pack[target, row] = rows.pop((target, row))
-
-    def depth_copy(step, group):
-        target = lax.rem(d + step, slabs)
-        start, stop = plan.groups[group]
-        part_rows = pl.ds(start, stop - start)
+    cores = 2 if slabs % 2 == 0 else 1
+
+    def peer(step, sign):
+        chip, core = d // cores, lax.rem(d, cores)
+        far, flip = step // cores, step % cores
+        chips = slabs // cores
+        return lax.rem(chip + chips + sign * far, chips) * cores + (1 - core if flip else core)
+
+    def depth_copy(step, kind):
+        source, target = (rim_pack, rim_held) if kind else (pack, held)
         if step == 0:
-            return pltpu.make_async_copy(
-                pack.at[d, part_rows], held.at[d, part_rows], dr_sem.at[0, group]
-            )
+            return pltpu.make_async_copy(source.at[d], target.at[d], dr_sem.at[0, kind])
+        to = peer(step, 1)
         return pltpu.make_async_remote_copy(
-            src_ref=pack.at[target, part_rows],
-            dst_ref=held.at[d, part_rows],
-            send_sem=ds_sem.at[step, group],
-            recv_sem=dr_sem.at[step, group],
-            device_id=(t, target),
+            src_ref=source.at[to],
+            dst_ref=target.at[d],
+            send_sem=ds_sem.at[step, kind],
+            recv_sem=dr_sem.at[step, kind],
+            device_id=(t, to),
             device_id_type=MESH,
         )
 
     def line_copy(source, n):
-        o, group, first, size, at = plan.pieces[source][n]
+        o, group, first, size, at, kind = plan.pieces[source][n]
         start, stop = plan.groups[group]
-        src = held.at[source, pl.ds(start, stop - start), pl.ds(first, size), :]
+        origin = rim_held if kind else held
+        src = origin.at[source, pl.ds(start, stop - start), pl.ds(first, size), :]
         dst = recv.at[source, pl.ds(start, stop - start), pl.ds(at, size), :]
         if o % tiles == 0:
             return pltpu.make_async_copy(src, dst, lr_sem.at[source, n]), False
@@ -397,38 +398,68 @@
             device_id_type=MESH,
         ), True
 
-    def forward(slab, group):
+    def forward(slab, kind):
         for source in range(slabs):
 
             @pl.when(slab == source)
             def _():
                 for n, piece in enumerate(plan.pieces[source]):
-                    if piece[1] == group:
+                    if piece[5] == kind:
                         line_copy(source, n)[0].start()
 
-    for group in range(groups):
-        x_copy(0, group).wait_recv()
-        x_copy(1, group).wait_recv()
-        for slot in range(*plan.spans[group]):
-            emit(slot)
-        for step in range(slabs):
-            depth_copy(step, group).start()
-        depth_copy(0, group).wait()
-        forward(d, group)
-
-    for group in range(groups):
-        for step in range(1, slabs):
-            depth_copy(step, group).wait_recv()
-            forward(lax.rem(d + slabs - step, slabs), group)
+    line_rows = (0, 1, 3, 4, 5, 6, 7)
+    x_row = {row: c for c, row in enumerate(ROWS[0])}
+
+    def core_state(slot):
+        level = order[slot]
+        out = []
+        for row in line_rows:
+            value = part[row, level, 3:width - 3, :]
+            if row in x_row:
+                value = value - stencil(
+                    [xf[x_row[row], slot, pl.ds(PAD + i, plan.core), :] for i in range(7)]
+                )
+            out.append(value)
+        return out
+
+    emit(core_state, pack, plan.core)
+    for step in range(slabs):
+        depth_copy(step, 0).start()
+    for step in range(slabs):
+        if step:
+            depth_copy(step, 0).wait_recv()
+        else:
+            depth_copy(step, 0).wait()
+        forward(peer(step, -1), 0)
+
+    x_copy(0, 0).wait_recv()
+    x_copy(1, 0).wait_recv()
+    low_rows = lax.broadcasted_iota(jnp.int32, (8, 128), 0) < 3
+
+    def rim_state(slot):
+        new = finish(slot)
+        return [
+            jnp.where(low_rows, new[row][:8], new[row][width - 8:]) for row in line_rows
+        ]
+
+    emit(rim_state, rim_pack, 8)
+    for step in range(slabs):
+        depth_copy(step, 1).start()
+    for step in range(slabs):
+        if step:
+            depth_copy(step, 1).wait_recv()
+        else:
+            depth_copy(step, 1).wait()
+        forward(peer(step, -1), 1)
 
     def rest(slot, carry):
         finish(slot)
         return carry
 
-    for span in range(groups, spans):
+    for span in range(1, spans):
         x_copy(0, span).wait_recv()
         x_copy(1, span).wait_recv()
-        lax.fori_loop(plan.spans[span][0], plan.spans[span][1], rest, 0)
+        lax.fori_loop(*plan.spans[span], rest, 0)
 
     for source in range(slabs):
         for n in range(len(plan.pieces[source])):
@@ -450,9 +481,9 @@
     def _():
         z_copy(1).wait_send()
 
-    for group in range(groups):
+    for kind in range(2):
         for step in range(1, slabs):
-            depth_copy(step, group).wait_send()
+            depth_copy(step, kind).wait_send()
     for source in range(slabs):
         for n in range(len(plan.pieces[source])):
             copy, remote = line_copy(source, n)
@@ -540,7 +571,7 @@
     vmem = pl.BlockSpec(memory_space=pltpu.VMEM)
     state_shape = (8, cells, width, cross)
     lines_shape = (slabs, plan.packed, plan.rows, 128)
-    parts, spans = len(plan.groups), len(plan.spans)
+    spans = len(plan.spans)
     state, lines, order = pl.pallas_call(
         functools.partial(section_kernel, plan),
         out_shape=(
@@ -557,15 +588,17 @@
             pltpu.VMEM((7, cells, width + 2 * PAD, cross), F32),
             pltpu.VMEM((7, cells + 6, width, cross), F32),
             pltpu.VMEM(state_shape, F32),
-            pltpu.VMEM((slabs, plan.packed, width, 128), F32),
-            pltpu.VMEM((slabs, plan.packed, width, 128), F32),
+            pltpu.VMEM((slabs, plan.packed, plan.core, 128), F32),
+            pltpu.VMEM((slabs, plan.packed, 8, 128), F32),
+            pltpu.VMEM((slabs, plan.packed, plan.core, 128), F32),
+            pltpu.VMEM((slabs, plan.packed, 8, 128), F32),
             pltpu.SemaphoreType.DMA((6,)),
             pltpu.SemaphoreType.DMA((2, spans)),
             pltpu.SemaphoreType.DMA((2, spans)),
             pltpu.SemaphoreType.DMA((2,)),
             pltpu.SemaphoreType.DMA((2,)),
-            pltpu.SemaphoreType.DMA((slabs, parts)),
-            pltpu.SemaphoreType.DMA((slabs, parts)),
+            pltpu.SemaphoreType.DMA((slabs, 2)),
+            pltpu.SemaphoreType.DMA((slabs, 2)),
             pltpu.SemaphoreType.DMA((slabs, plan.count)),
             pltpu.SemaphoreType.DMA((slabs, plan.count)),
         ],
@@ -603,7 +636,7 @@
 
     def body(density, momentum, magnetic, energy, shifts, levels):
         cells, width, cross = density.shape
-        plan = Plan(tiles, slabs, cells, width, cross, levels.shape[0], 2)
+        plan = Plan(tiles, slabs, cells, width, cross, levels.shape[0], 1)
         return per_device(plan, density, momentum, magnetic, energy, shifts, levels)
 
     return jax.shard_map(

time: 27.4 us -> 26.6 us (0.971)
  Pallas kernels: 26.6 us -> 25.8 us
    pallas_call x1, Pallas kernels: 23.4 us -> 22.6 us  [per_device(): pl.pallas_call(functools.partial(section_kernel, plan), out_shape=(pltpu....]
where the time goes in v4:
time: 26.6 us; the launch traced here: 26.5 us
  Pallas kernels  25.8 us (97%)
  between operations  0.64 us (2%)
    pallas_call x1, Pallas kernels, per_device(): pl.pallas_call(functools.partial(section_kernel, plan), out_shape=(pltpu....  22.6 us
    pallas_call x1, Pallas kernels, per_device(): pl.pallas_call(functools.partial(ray_kernel, plan), out_shape=(jax.ShapeD...  3.24 us

profile of v4, /device:TPU:0, one launch (start us, length us, event | category | flops | bytes accessed | tf_op | source)
XLA Modules:
  0.0 26.5 jit_solution(7697244940978744793)
XLA Ops:
  0.6 22.6 %section.1 = (f32[8,16,16,128]{3,2,1,0:T(8,128)S(1)}, f32[4,6,32,128]{3,2,1,0:T(8,128)S(1)}, s32[88]{0:T(128)S(1)}) custom-call(s32[24]{0:T(128)} %levels_in.1, s32[24]{0:T(128)} %shifts_in.1, f32[16,16,128]{2,1,0:T(8,128)} %density.1, f32[3,16,16,128]{3,2,1,0:T(8,128)} %momentum.1, f32[3,16,16,128]{3,2,1,0:T(8,128)} %magnetic.1, f32[16,16,128]{2,1,0:T(8,128)} %energy.1), custom_call_target="tpu_custom_call" | custom-call | tf_op jit(solution)/shard_map/section/pallas_call | solution.py:575
  23.2 3.2 %ray.1 = (f32[8,16,16,128]{3,2,1,0:T(8,128)}, f32[512,48]{1,0:T(8,128)}) custom-call(s32[88]{0:T(128)S(1)} %get-tuple-element.7.order, f32[4,6,32,128]{3,2,1,0:T(8,128)S(1)} %get-tuple-element.8.rows, f32[8,16,16,128]{3,2,1,0:T(8,128)S(1)} %get-tuple-element.9.hold), custom_call_target="tpu_custom_call" | custom-call | tf_op jit(solution)/shard_map/ray/pallas_call | solution.py:615

commit v5 on v4

--- a/solution.py
+++ b/solution.py
@@ -161,8 +161,9 @@
 
 def section_kernel(
     plan, levels_in, shifts_in, density, momentum, magnetic, energy, ns, recv, order,
-    levels, shifts, st, xf, zf, part, pack, rim_pack, held, rim_held,
+    levels, shifts, st, xf, yf, zf, part, pack, rim_pack, held, rim_held,
     in_sem, xs_sem, xr_sem, zs_sem, zr_sem, ds_sem, dr_sem, ls_sem, lr_sem,
+    rs_sem,
 ):
     tiles, slabs, cells, width = plan.tiles, plan.slabs, plan.depth_cells, plan.width
     most = plan.most
@@ -236,47 +237,6 @@
 
     spans = len(plan.spans)
 
-    def along_z(level):
-        values = flux_along(2, primitives(st, level))
-        for c in range(7):
-            zf[c, level + 3] = values[c]
-
-    def rim(i, carry):
-        along_z(i)
-        along_z(cells - 3 + i)
-        return carry
-
-    lax.fori_loop(0, 3, rim, 0)
-    lax.fori_loop(*plan.spans[0], along_x, 0)
-    pl.semaphore_wait(barrier, 2 + (slabs - 1) + len(plan.reach))
-
-    @pl.when(d < slabs - 1)
-    def _():
-        z_copy(0).start()
-
-    @pl.when(d > 0)
-    def _():
-        z_copy(1).start()
-
-    x_copy(0, 0).start()
-    x_copy(1, 0).start()
-    for span in range(1, spans):
-        lax.fori_loop(*plan.spans[span], along_x, 0)
-        x_copy(0, span).start()
-        x_copy(1, span).start()
-
-    def inner(level, carry):
-        along_z(level)
-        return carry
-
-    lax.fori_loop(3, cells - 3, inner, 0)
-
-    def cross(f):
-        def at(step):
-            return pltpu.roll(f, (-step) % plan.cross, 1)
-
-        return stencil([at(i - 3) if i != 3 else f for i in range(7)])
-
     def along_y(level, carry):
         values = primitives(st, level)
         rho, m, b, _, en, _, _ = values
@@ -284,14 +244,77 @@
             rho, m[0], m[1], m[2] + (SECTION * GRAVITY) * rho, b[0], b[1], b[2],
             en + (SECTION * GRAVITY) * m[2],
         ]
-        flux = flux_along(1, values)
-        for c, row in enumerate(ROWS[1]):
-            base[row] = base[row] - cross(flux[c])
         for row in range(8):
             part[row, level] = base[row]
+        for c, f in enumerate(flux_along(1, values)):
+            high = f.astype(jnp.bfloat16)
+            yf[c, level, :, :plan.cross] = high
+            yf[c, level, :, plan.cross:] = (f - high.astype(F32)).astype(jnp.bfloat16)
         return carry
 
-    lax.fori_loop(0, cells, along_y, 0)
+    def cross():
+        shape = (2 * plan.cross, plan.cross)
+        ahead = lax.broadcasted_iota(jnp.int32, shape, 0) - lax.broadcasted_iota(
+            jnp.int32, shape, 1
+        )
+        ahead = lax.rem(ahead + plan.cross, plan.cross)
+        band = jnp.zeros(shape, F32)
+        for i, weight in ((1, 45.0), (2, -9.0), (3, 1.0)):
+            band = jnp.where(ahead == i, weight, band)
+            band = jnp.where(ahead == plan.cross - i, -weight, band)
+        band = band.astype(jnp.bfloat16)
+        for c, row in enumerate(ROWS[1]):
+            flat = yf[c].reshape(cells * width, 2 * plan.cross)
+            slope = jnp.dot(flat, band, preferred_element_type=F32)
+            part[row] = part[row] - SCALE * slope.reshape(cells, width, plan.cross)
+
+    def all_y():
+        lax.fori_loop(0, cells, along_y, 0)
+        cross()
+
+    def early(work):
+        pass
+
+    def late(work):
+        work()
+
+    def along_z(level):
+        values = flux_along(2, primitives(st, level))
+        for c in range(7):
+            zf[c, level + 3] = values[c]
+
+    def rim(i, carry):
+        along_z(i)
+        along_z(cells - 3 + i)
+        return carry
+
+    lax.fori_loop(0, 3, rim, 0)
+    lax.fori_loop(*plan.spans[0], along_x, 0)
+    early(all_y)
+    pl.semaphore_wait(barrier, 2 + (slabs - 1) + len(plan.reach))
+
+    @pl.when(d < slabs - 1)
+    def _():
+        z_copy(0).start()
+
+    @pl.when(d > 0)
+    def _():
+        z_copy(1).start()
+
+    x_copy(0, 0).start()
+    x_copy(1, 0).start()
+    for span in range(1, spans):
+        lax.fori_loop(*plan.spans[span], along_x, 0)
+        x_copy(0, span).start()
+        x_copy(1, span).start()
+
+    def inner(level, carry):
+        along_z(level)
+        return carry
+
+    lax.fori_loop(3, cells - 3, inner, 0)
+
+    late(all_y)
 
     @pl.when(d == 0)
     def _():
@@ -369,8 +392,6 @@
 
     def depth_copy(step, kind):
         source, target = (rim_pack, rim_held) if kind else (pack, held)
-        if step == 0:
-            return pltpu.make_async_copy(source.at[d], target.at[d], dr_sem.at[0, kind])
         to = peer(step, 1)
         return pltpu.make_async_remote_copy(
             src_ref=source.at[to],
@@ -381,31 +402,56 @@
             device_id_type=MESH,
         )
 
-    def line_copy(source, n):
+    def line_copy(source, n, own=False):
         o, group, first, size, at, kind = plan.pieces[source][n]
         start, stop = plan.groups[group]
-        origin = rim_held if kind else held
-        src = origin.at[source, pl.ds(start, stop - start), pl.ds(first, size), :]
-        dst = recv.at[source, pl.ds(start, stop - start), pl.ds(at, size), :]
-        if o % tiles == 0:
-            return pltpu.make_async_copy(src, dst, lr_sem.at[source, n]), False
+        if own:
+            origin = rim_pack if kind else pack
+        else:
+            origin = rim_held if kind else held
         return pltpu.make_async_remote_copy(
-            src_ref=src,
-            dst_ref=dst,
+            src_ref=origin.at[source, pl.ds(start, stop - start), pl.ds(first, size), :],
+            dst_ref=recv.at[source, pl.ds(start, stop - start), pl.ds(at, size), :],
             send_sem=ls_sem.at[source, n],
             recv_sem=lr_sem.at[source, n],
             device_id=(lax.rem(t + tiles - o % tiles, tiles), d),
             device_id_type=MESH,
-        ), True
-
-    def forward(slab, kind):
+        )
+
+    def rim_copy(source, n, target):
+        o, group, first, size, at, _ = plan.pieces[source][n]
+        start, stop = plan.groups[group]
+        return pltpu.make_async_remote_copy(
+            src_ref=rim_pack.at[target, pl.ds(start, stop - start), pl.ds(first, size), :],
+            dst_ref=recv.at[source, pl.ds(start, stop - start), pl.ds(at, size), :],
+            send_sem=rs_sem.at[n, target],
+            recv_sem=lr_sem.at[source, n],
+            device_id=(lax.rem(t + tiles - o % tiles, tiles), target),
+            device_id_type=MESH,
+        )
+
+    def keep(source, n, own):
+        _, group, first, size, at, kind = plan.pieces[source][n]
+        start, stop = plan.groups[group]
+        if own:
+            origin = rim_pack if kind else pack
+        else:
+            origin = rim_held if kind else held
+        for row in range(start, stop):
+            recv[source, row, at:at + size, :] = origin[source, row, first:first + size, :]
+
+    def forward(slab, kind, own=False):
         for source in range(slabs):
 
             @pl.when(slab == source)
             def _():
-                for n, piece in enumerate(plan.pieces[source]):
-                    if piece[5] == kind:
-                        line_copy(source, n)[0].start()
+                for stays in (False, True):
+                    for n, piece in enumerate(plan.pieces[source]):
+                        if piece[5] == kind and (piece[0] % tiles == 0) == stays:
+                            if stays:
+                                keep(source, n, own)
+                            else:
+                                line_copy(source, n, own).start()
 
     line_rows = (0, 1, 3, 4, 5, 6, 7)
     x_row = {row: c for c, row in enumerate(ROWS[0])}
@@ -423,13 +469,11 @@
         return out
 
     emit(core_state, pack, plan.core)
-    for step in range(slabs):
+    for step in range(1, slabs):
         depth_copy(step, 0).start()
-    for step in range(slabs):
-        if step:
-            depth_copy(step, 0).wait_recv()
-        else:
-            depth_copy(step, 0).wait()
+    forward(d, 0, own=True)
+    for step in range(1, slabs):
+        depth_copy(step, 0).wait_recv()
         forward(peer(step, -1), 0)
 
     x_copy(0, 0).wait_recv()
@@ -443,14 +487,24 @@
         ]
 
     emit(rim_state, rim_pack, 8)
-    for step in range(slabs):
-        depth_copy(step, 1).start()
-    for step in range(slabs):
-        if step:
-            depth_copy(step, 1).wait_recv()
-        else:
-            depth_copy(step, 1).wait()
-        forward(peer(step, -1), 1)
+    rims = [
+        (source, n)
+        for source in range(slabs)
+        for n, piece in enumerate(plan.pieces[source])
+        if piece[5] == 1
+    ]
+    for source in range(slabs):
+
+        @pl.when(d == source)
+        def _():
+            for one, n in rims:
+                if one == source:
+                    for target in range(slabs):
+                        if target == source and plan.pieces[source][n][0] % tiles == 0:
+                            keep(source, n, True)
+                        else:
+                            rim_copy(source, n, target).start()
+
 
     def rest(slot, carry):
         finish(slot)
@@ -463,11 +517,13 @@
 
     for source in range(slabs):
         for n in range(len(plan.pieces[source])):
-            copy, remote = line_copy(source, n)
-            if remote:
-                copy.wait_recv()
-            else:
-                copy.wait()
+            here = plan.pieces[source][n][0] % tiles == 0
+            if plan.pieces[source][n][5] == 1 and here:
+                pl.when(d != source)(rim_copy(source, n, source).wait_recv)
+            elif plan.pieces[source][n][5] == 1:
+                rim_copy(source, n, source).wait_recv()
+            elif not here:
+                line_copy(source, n).wait_recv()
 
     for span in range(spans):
         x_copy(0, span).wait_send()
@@ -481,14 +537,20 @@
     def _():
         z_copy(1).wait_send()
 
-    for kind in range(2):
-        for step in range(1, slabs):
-            depth_copy(step, kind).wait_send()
+    for step in range(1, slabs):
+        depth_copy(step, 0).wait_send()
     for source in range(slabs):
         for n in range(len(plan.pieces[source])):
-            copy, remote = line_copy(source, n)
-            if remote:
-                copy.wait_send()
+            if plan.pieces[source][n][0] % tiles and plan.pieces[source][n][5] == 0:
+                line_copy(source, n).wait_send()
+
+        @pl.when(d == source)
+        def _():
+            for one, n in rims:
+                if one == source:
+                    for target in range(slabs):
+                        if not (target == source and plan.pieces[source][n][0] % tiles == 0):
+                            rim_copy(source, n, target).wait_send()
 
 
 def ray_kernel(plan, order, rows, hold, state_out, intensity, fields, out_sem):
@@ -586,6 +648,7 @@
             pltpu.SMEM((plan.positions,), jnp.int32),
             pltpu.VMEM(state_shape, F32),
             pltpu.VMEM((7, cells, width + 2 * PAD, cross), F32),
+            pltpu.VMEM((7, cells, width, 2 * cross), jnp.bfloat16),
             pltpu.VMEM((7, cells + 6, width, cross), F32),
             pltpu.VMEM(state_shape, F32),
             pltpu.VMEM((slabs, plan.packed, plan.core, 128), F32),
@@ -601,6 +664,7 @@
             pltpu.SemaphoreType.DMA((slabs, 2)),
             pltpu.SemaphoreType.DMA((slabs, plan.count)),
             pltpu.SemaphoreType.DMA((slabs, plan.count)),
+            pltpu.SemaphoreType.DMA((plan.count, slabs)),
         ],
         compiler_params=pltpu.CompilerParams(
             collective_id=0, has_side_effects=True, vmem_limit_bytes=16 << 20

time: 26.6 us -> 26 us (0.977)
  Pallas kernels: 25.8 us -> 25.1 us
    pallas_call x1, Pallas kernels: 22.6 us -> 21.9 us  [per_device(): pl.pallas_call(functools.partial(section_kernel, plan), out_shape=(pltpu....]
where the time goes in v5:
time: 26 us; the launch traced here: 25.8 us
  Pallas kernels  25.1 us (97%)
  between operations  0.64 us (2%)
    pallas_call x1, Pallas kernels, per_device(): pl.pallas_call(functools.partial(section_kernel, plan), out_shape=(pltpu....  21.9 us
    pallas_call x1, Pallas kernels, per_device(): pl.pallas_call(functools.partial(ray_kernel, plan), out_shape=(jax.ShapeD...  3.24 us

profile of v5, /device:TPU:0, one launch (start us, length us, event | category | flops | bytes accessed | tf_op | source)
XLA Modules:
  0.0 25.8 jit_solution(15070827501075214741)
XLA Ops:
  0.6 21.9 %section.1 = (f32[8,16,16,128]{3,2,1,0:T(8,128)S(1)}, f32[4,6,32,128]{3,2,1,0:T(8,128)S(1)}, s32[88]{0:T(128)S(1)}) custom-call(s32[24]{0:T(128)} %levels_in.1, s32[24]{0:T(128)} %shifts_in.1, f32[16,16,128]{2,1,0:T(8,128)} %density.1, f32[3,16,16,128]{3,2,1,0:T(8,128)} %momentum.1, f32[3,16,16,128]{3,2,1,0:T(8,128)} %magnetic.1, f32[16,16,128]{2,1,0:T(8,128)} %energy.1), custom_call_target="tpu_custom_call" | custom-call | tf_op jit(solution)/shard_map/section/pallas_call | solution.py:637
  22.5 3.2 %ray.1 = (f32[8,16,16,128]{3,2,1,0:T(8,128)}, f32[512,48]{1,0:T(8,128)}) custom-call(s32[88]{0:T(128)S(1)} %get-tuple-element.7.order, f32[4,6,32,128]{3,2,1,0:T(8,128)S(1)} %get-tuple-element.8.rows, f32[8,16,16,128]{3,2,1,0:T(8,128)S(1)} %get-tuple-element.9.hold), custom_call_target="tpu_custom_call" | custom-call | tf_op jit(solution)/shard_map/ray/pallas_call | solution.py:679

commit v6 on v5

--- a/solution.py
+++ b/solution.py
@@ -105,6 +105,14 @@
         order[j] = jnp.clip(jnp.where(j < full, j, later), 0, cells - 1)
     for j in range(cells - most):
         order[most + j] = jnp.clip(free(spare + j), 0, cells - 1)
+    first = [order[j] for j in range(most)]
+    for level in range(cells):
+        below, here = jnp.int32(0), jnp.int32(0)
+        for one in first:
+            below = below + jnp.where(one < level, 1, 0)
+            here = here + jnp.where(one == level, 1, 0)
+        slot = jnp.where(here > 0, below, most + level - below)
+        order[cells + 3 * positions + level] = jnp.clip(slot, 0, cells - 1)
 
 
 def ray_order(plan, levels, shifts, order):
@@ -119,9 +127,10 @@
     for k in range(positions):
         spare = jnp.minimum(most - held[k], levels[k] - slab[k] * cells - before[k])
         at = cells + 3 * k
-        order[at] = slab[k]
-        order[at + 1] = before[k] + spare
-        order[at + 2] = shifts[k] - (1732 * (slab[k] * cells) + 1000) // 2000
+        start = shifts[k] - (1732 * (slab[k] * cells) + 1000) // 2000
+        order[at] = jnp.clip(slab[k], 0, plan.slabs - 1)
+        order[at + 1] = jnp.clip(before[k] + spare, 0, most - 1)
+        order[at + 2] = jnp.clip(start, 0, plan.rows - plan.width)
 
 
 def primitives(st, level):
@@ -160,8 +169,8 @@
 
 
 def section_kernel(
-    plan, levels_in, shifts_in, density, momentum, magnetic, energy, ns, recv, order,
-    levels, shifts, st, xf, yf, zf, part, pack, rim_pack, held, rim_held,
+    plan, levels_in, shifts_in, density, momentum, magnetic, energy, ns, fields,
+    order, recv, levels, shifts, st, xf, yf, zf, part, pack, rim_pack, held, rim_held,
     in_sem, xs_sem, xr_sem, zs_sem, zr_sem, ds_sem, dr_sem, ls_sem, lr_sem,
     rs_sem,
 ):
@@ -346,20 +355,15 @@
     lax.fori_loop(0, cells, depth_part, 0)
     ray_order(plan, levels, shifts, order)
 
-    def finish(slot):
-        level = order[slot]
-        row_of = {row: c for c, row in enumerate(ROWS[0])}
-        out = []
-        for row in range(8):
-            value = part[row, level]
-            if row in row_of:
-                c = row_of[row]
-                value = value - stencil(
-                    [xf[c, slot, pl.ds(PAD - 3 + i, width), :] for i in range(7)]
-                )
-            ns[row, slot] = value
-            out.append(value)
-        return out
+    x_row = {row: c for c, row in enumerate(ROWS[0])}
+
+    def advance(row, level, slot):
+        value = part[row, level]
+        if row in x_row:
+            value = value - stencil(
+                [xf[x_row[row], slot, pl.ds(PAD - 3 + i, width), :] for i in range(7)]
+            )
+        return value
 
     def emit(new, out, height):
         block_of = lax.broadcasted_iota(jnp.int32, (height, 128), 1) // plan.lanes
@@ -454,7 +458,6 @@
                                 line_copy(source, n, own).start()
 
     line_rows = (0, 1, 3, 4, 5, 6, 7)
-    x_row = {row: c for c, row in enumerate(ROWS[0])}
 
     def core_state(slot):
         level = order[slot]
@@ -481,10 +484,8 @@
     low_rows = lax.broadcasted_iota(jnp.int32, (8, 128), 0) < 3
 
     def rim_state(slot):
-        new = finish(slot)
-        return [
-            jnp.where(low_rows, new[row][:8], new[row][width - 8:]) for row in line_rows
-        ]
+        new = [advance(row, order[slot], slot) for row in line_rows]
+        return [jnp.where(low_rows, one[:8], one[width - 8:]) for one in new]
 
     emit(rim_state, rim_pack, 8)
     rims = [
@@ -506,14 +507,16 @@
                             rim_copy(source, n, target).start()
 
 
-    def rest(slot, carry):
-        finish(slot)
+    def rest(level, carry):
+        slot = order[cells + 3 * plan.positions + level]
+        for row in range(8):
+            ns[row, level] = advance(row, level, slot)
         return carry
 
     for span in range(1, spans):
         x_copy(0, span).wait_recv()
         x_copy(1, span).wait_recv()
-        lax.fori_loop(*plan.spans[span], rest, 0)
+    lax.fori_loop(0, cells, rest, 0)
 
     for source in range(slabs):
         for n in range(len(plan.pieces[source])):
@@ -525,6 +528,30 @@
             elif not here:
                 line_copy(source, n).wait_recv()
 
+    lane = lax.broadcasted_iota(jnp.int32, (width, 128), 1)
+    within = lax.rem(lane, plan.lanes)
+    wanted = lane // plan.lanes == lax.rem(
+        lax.broadcasted_iota(jnp.int32, (width, 128), 0), plan.blocks
+    )
+    for k in range(plan.positions):
+        at = cells + 3 * k
+        slab, slot, start = order[at], order[at + 1], order[at + 2]
+        for f in range(3):
+            item = 3 * slot + f
+            row, block = item // plan.blocks, lax.rem(item, plan.blocks)
+            value = recv[slab, row, pl.ds(start, width), :]
+            value = jnp.take_along_axis(value, within + block * plan.lanes, axis=1)
+            value = jnp.where(wanted, value, 0.0)
+            step = 1
+            while step < plan.blocks:
+                value = value + pltpu.roll(value, width - step, 0)
+                step *= 2
+            if f == 0:
+                value = value * (-LOG2E * 2.0 / plan.positions)
+            elif f == 1:
+                value = value * ROOT_LOG2E
+            fields[f, k] = value
+
     for span in range(spans):
         x_copy(0, span).wait_send()
         x_copy(1, span).wait_send()
@@ -553,39 +580,10 @@
                             rim_copy(source, n, target).wait_send()
 
 
-def ray_kernel(plan, order, rows, hold, state_out, intensity, fields, out_sem):
-    cells, width, blocks = plan.depth_cells, plan.width, plan.blocks
-    lanes, positions = plan.lanes, plan.positions
-    out_copies = [
-        pltpu.make_async_copy(hold.at[:, j], state_out.at[:, order[j]], out_sem.at[j])
-        for j in range(cells)
-    ]
-    for copy in out_copies:
-        copy.start()
-
-    lane = lax.broadcasted_iota(jnp.int32, (width, 128), 1)
-    within = lax.rem(lane, lanes)
-    wanted = lane // lanes == lax.rem(
-        lax.broadcasted_iota(jnp.int32, (width, 128), 0), blocks
-    )
-    for k in range(positions):
-        at = cells + 3 * k
-        slab, slot, start = order[at], order[at + 1], order[at + 2]
-        for f in range(3):
-            item = 3 * slot + f
-            row, block = item // blocks, lax.rem(item, blocks)
-            value = rows[slab, row, pl.ds(start, width), :]
-            value = jnp.take_along_axis(value, within + block * lanes, axis=1)
-            value = jnp.where(wanted, value, 0.0)
-            step = 1
-            while step < blocks:
-                value = value + pltpu.roll(value, width - step, 0)
-                step *= 2
-            if f == 0:
-                value = value * (-LOG2E * 2.0 / positions)
-            elif f == 1:
-                value = value * ROOT_LOG2E
-            fields[f, k] = value
+def ray_kernel(plan, fields, hold, state_out, intensity, out_sem):
+    width, blocks, positions = plan.width, plan.blocks, plan.positions
+    out_copy = pltpu.make_async_copy(hold, state_out, out_sem)
+    out_copy.start()
 
     groups = W // 8
     for part in range(width // blocks):
@@ -616,34 +614,34 @@
 
         ones = tuple(jnp.ones((8, 128), F32) for _ in range(groups))
         zeros = tuple(jnp.zeros((8, 128), F32) for _ in range(groups))
-        seen, total = lax.fori_loop(0, positions, step, (ones, zeros), unroll=8)
+        seen, total = lax.fori_loop(0, positions, step, (ones, zeros), unroll=24)
         last = field(2, positions - 1)
         value = jnp.concatenate([total[g] + last * seen[g] for g in range(groups)], axis=0)
         intensity[part * 128:(part + 1) * 128, :] = value.T
 
-    for copy in out_copies:
-        copy.wait()
+    out_copy.wait()
 
 
 def per_device(plan, density, momentum, magnetic, energy, shifts, levels):
     cells, width, cross = density.shape
     slabs = plan.slabs
     any_spec = pl.BlockSpec(memory_space=pl.ANY)
-    scalars = pl.BlockSpec(memory_space=pltpu.SMEM)
     vmem = pl.BlockSpec(memory_space=pltpu.VMEM)
     state_shape = (8, cells, width, cross)
     lines_shape = (slabs, plan.packed, plan.rows, 128)
+    fields_shape = (3, plan.positions, width, 128)
     spans = len(plan.spans)
-    state, lines, order = pl.pallas_call(
+    state, fields = pl.pallas_call(
         functools.partial(section_kernel, plan),
         out_shape=(
             pltpu.VMEM(state_shape, F32),
-            pltpu.VMEM(lines_shape, F32),
-            jax.ShapeDtypeStruct((cells + 3 * plan.positions,), jnp.int32),
+            pltpu.VMEM(fields_shape, F32),
         ),
         in_specs=[pl.BlockSpec(memory_space=pltpu.HBM)] * 6,
-        out_specs=(vmem, vmem, scalars),
+        out_specs=(vmem, vmem),
         scratch_shapes=[
+            pltpu.SMEM((2 * cells + 3 * plan.positions,), jnp.int32),
+            pltpu.VMEM(lines_shape, F32),
             pltpu.SMEM((plan.positions,), jnp.int32),
             pltpu.SMEM((plan.positions,), jnp.int32),
             pltpu.VMEM(state_shape, F32),
@@ -674,7 +672,7 @@
         pltpu.with_memory_space_constraint(x, pltpu.HBM)
         for x in (levels, shifts, density, momentum, magnetic, energy)
     ))
-    lines = pltpu.with_memory_space_constraint(lines, pltpu.VMEM)
+    fields = pltpu.with_memory_space_constraint(fields, pltpu.VMEM)
     state = pltpu.with_memory_space_constraint(state, pltpu.VMEM)
     new_state, intensity = pl.pallas_call(
         functools.partial(ray_kernel, plan),
@@ -682,15 +680,14 @@
             jax.ShapeDtypeStruct(state_shape, F32),
             jax.ShapeDtypeStruct((width * plan.lanes, W), F32),
         ),
-        in_specs=[scalars, vmem, vmem],
+        in_specs=[vmem, vmem],
         out_specs=(any_spec, vmem),
         scratch_shapes=[
-            pltpu.VMEM((3, plan.positions, width, 128), F32),
-            pltpu.SemaphoreType.DMA((cells,)),
+            pltpu.SemaphoreType.DMA,
         ],
         compiler_params=pltpu.CompilerParams(vmem_limit_bytes=16 << 20),
         name="ray",
-    )(order, lines, state)
+    )(fields, state)
     intensity = intensity.reshape(width, plan.lanes, W)
     return new_state, jnp.transpose(intensity, (2, 0, 1))
 

time: 26 us -> 24.5 us (0.942)
  Pallas kernels: 25.1 us -> 23.6 us
    pallas_call x1, Pallas kernels: 3.24 us -> 1.78 us  [per_device(): pl.pallas_call(functools.partial(ray_kernel, plan), out_shape=(jax.ShapeD...]
where the time goes in v6:
time: 24.5 us; the launch traced here: 24.3 us
  Pallas kernels  23.6 us (96%)
  between operations  0.64 us (3%)
    pallas_call x1, Pallas kernels, per_device(): pl.pallas_call(functools.partial(section_kernel, plan), out_shape=(pltpu....  21.9 us
    pallas_call x1, Pallas kernels, per_device(): pl.pallas_call(functools.partial(ray_kernel, plan), out_shape=(jax.ShapeD...  1.78 us

profile of v6, /device:TPU:0, one launch (start us, length us, event | category | flops | bytes accessed | tf_op | source)
XLA Modules:
  0.0 24.3 jit_solution(14149361904457789207)
XLA Ops:
  0.6 21.9 %section.1 = (f32[8,16,16,128]{3,2,1,0:T(8,128)S(1)}, f32[3,24,16,128]{3,2,1,0:T(8,128)S(1)}) custom-call(s32[24]{0:T(128)} %levels_in.1, s32[24]{0:T(128)} %shifts_in.1, f32[16,16,128]{2,1,0:T(8,128)} %density.1, f32[3,16,16,128]{3,2,1,0:T(8,128)} %momentum.1, f32[3,16,16,128]{3,2,1,0:T(8,128)} %magnetic.1, f32[16,16,128]{2,1,0:T(8,128)} %energy.1), custom_call_target="tpu_custom_call" | custom-call | tf_op jit(solution)/shard_map/section/pallas_call | solution.py:634
  22.5 1.8 %ray.1 = (f32[8,16,16,128]{3,2,1,0:T(8,128)}, f32[512,48]{1,0:T(8,128)}) custom-call(f32[3,24,16,128]{3,2,1,0:T(8,128)S(1)} %get-tuple-element.6.fields, f32[8,16,16,128]{3,2,1,0:T(8,128)S(1)} %get-tuple-element.7.hold), custom_call_target="tpu_custom_call" | custom-call | tf_op jit(solution)/shard_map/ray/pallas_call | solution.py:677

commit v7 on v6

--- a/solution.py
+++ b/solution.py
@@ -281,12 +281,6 @@
         lax.fori_loop(0, cells, along_y, 0)
         cross()
 
-    def early(work):
-        pass
-
-    def late(work):
-        work()
-
     def along_z(level):
         values = flux_along(2, primitives(st, level))
         for c in range(7):
@@ -299,7 +293,6 @@
 
     lax.fori_loop(0, 3, rim, 0)
     lax.fori_loop(*plan.spans[0], along_x, 0)
-    early(all_y)
     pl.semaphore_wait(barrier, 2 + (slabs - 1) + len(plan.reach))
 
     @pl.when(d < slabs - 1)
@@ -323,7 +316,7 @@
 
     lax.fori_loop(3, cells - 3, inner, 0)
 
-    late(all_y)
+    all_y()
 
     @pl.when(d == 0)
     def _():
@@ -450,7 +443,7 @@
             @pl.when(slab == source)
             def _():
                 for stays in (False, True):
-                    for n, piece in enumerate(plan.pieces[source]):
+                    for n, piece in reversed(list(enumerate(plan.pieces[source]))):
                         if piece[5] == kind and (piece[0] % tiles == 0) == stays:
                             if stays:
                                 keep(source, n, own)
@@ -498,7 +491,7 @@
 
         @pl.when(d == source)
         def _():
-            for one, n in rims:
+            for one, n in reversed(rims):
                 if one == source:
                     for target in range(slabs):
                         if target == source and plan.pieces[source][n][0] % tiles == 0:
@@ -517,6 +510,33 @@
         x_copy(0, span).wait_recv()
         x_copy(1, span).wait_recv()
     lax.fori_loop(0, cells, rest, 0)
+
+    for span in range(spans):
+        x_copy(0, span).wait_send()
+        x_copy(1, span).wait_send()
+
+    @pl.when(d < slabs - 1)
+    def _():
+        z_copy(0).wait_send()
+
+    @pl.when(d > 0)
+    def _():
+        z_copy(1).wait_send()
+
+    for step in range(1, slabs):
+        depth_copy(step, 0).wait_send()
+    for source in range(slabs):
+        for n in range(len(plan.pieces[source])):
+            if plan.pieces[source][n][0] % tiles and plan.pieces[source][n][5] == 0:
+                line_copy(source, n).wait_send()
+
+        @pl.when(d == source)
+        def _():
+            for one, n in rims:
+                if one == source:
+                    for target in range(slabs):
+                        if not (target == source and plan.pieces[source][n][0] % tiles == 0):
+                            rim_copy(source, n, target).wait_send()
 
     for source in range(slabs):
         for n in range(len(plan.pieces[source])):
@@ -551,33 +571,6 @@
             elif f == 1:
                 value = value * ROOT_LOG2E
             fields[f, k] = value
-
-    for span in range(spans):
-        x_copy(0, span).wait_send()
-        x_copy(1, span).wait_send()
-
-    @pl.when(d < slabs - 1)
-    def _():
-        z_copy(0).wait_send()
-
-    @pl.when(d > 0)
-    def _():
-        z_copy(1).wait_send()
-
-    for step in range(1, slabs):
-        depth_copy(step, 0).wait_send()
-    for source in range(slabs):
-        for n in range(len(plan.pieces[source])):
-            if plan.pieces[source][n][0] % tiles and plan.pieces[source][n][5] == 0:
-                line_copy(source, n).wait_send()
-
-        @pl.when(d == source)
-        def _():
-            for one, n in rims:
-                if one == source:
-                    for target in range(slabs):
-                        if not (target == source and plan.pieces[source][n][0] % tiles == 0):
-                            rim_copy(source, n, target).wait_send()
 
 
 def ray_kernel(plan, fields, hold, state_out, intensity, out_sem):

time: 24.5 us -> 24.4 us (level)
  no operation moved by 1% of the time
where the time goes in v7:
time: 24.4 us; the launch traced here: 24.2 us
  Pallas kernels  23.6 us (97%)
  between operations  0.64 us (3%)
    pallas_call x1, Pallas kernels, per_device(): pl.pallas_call(functools.partial(section_kernel, plan), out_shape=(pltpu....  21.8 us
    pallas_call x1, Pallas kernels, per_device(): pl.pallas_call(functools.partial(ray_kernel, plan), out_shape=(jax.ShapeD...  1.78 us

profile of v7, /device:TPU:0, one launch (start us, length us, event | category | flops | bytes accessed | tf_op | source)
XLA Modules:
  0.0 24.2 jit_solution(17829972867382739727)
XLA Ops:
  0.6 21.8 %section.1 = (f32[8,16,16,128]{3,2,1,0:T(8,128)S(1)}, f32[3,24,16,128]{3,2,1,0:T(8,128)S(1)}) custom-call(s32[24]{0:T(128)} %levels_in.1, s32[24]{0:T(128)} %shifts_in.1, f32[16,16,128]{2,1,0:T(8,128)} %density.1, f32[3,16,16,128]{3,2,1,0:T(8,128)} %momentum.1, f32[3,16,16,128]{3,2,1,0:T(8,128)} %magnetic.1, f32[16,16,128]{2,1,0:T(8,128)} %energy.1), custom_call_target="tpu_custom_call" | custom-call | tf_op jit(solution)/shard_map/section/pallas_call | solution.py:627
  22.5 1.8 %ray.1 = (f32[8,16,16,128]{3,2,1,0:T(8,128)}, f32[512,48]{1,0:T(8,128)}) custom-call(f32[3,24,16,128]{3,2,1,0:T(8,128)S(1)} %get-tuple-element.6.fields, f32[8,16,16,128]{3,2,1,0:T(8,128)S(1)} %get-tuple-element.7.hold), custom_call_target="tpu_custom_call" | custom-call | tf_op jit(solution)/shard_map/ray/pallas_call | solution.py:670

commit v8 on v7

--- a/solution.py
+++ b/solution.py
@@ -52,6 +52,9 @@
         if depth_cells > self.most:
             self.spans.append((self.most, depth_cells))
         self.core = width - 6
+        self.sends = [(0, 6, 0, self.most), (6, 1, 0, self.most)]
+        if depth_cells > self.most:
+            self.sends.append((0, 7, self.most, depth_cells - self.most))
         self.pieces = []
         for d in range(slabs):
             mine = []
@@ -161,6 +164,7 @@
 
 
 ROWS = ((0, 1, 2, 3, 5, 6, 7), (0, 1, 2, 3, 4, 6, 7), (0, 1, 2, 3, 4, 5, 7))
+X_ROWS = (0, 1, 3, 5, 6, 7, 2)
 SCALE = SECTION / 60.0
 
 
@@ -214,18 +218,18 @@
 
     def along_x(slot, carry):
         values = flux_along(0, primitives(st, order[slot]))
-        for c in range(7):
-            xf[c, slot, PAD:PAD + width, :] = values[c]
+        for c, row in enumerate(X_ROWS):
+            xf[c, slot, PAD:PAD + width, :] = values[ROWS[0].index(row)]
         return carry
 
     def x_copy(side, span):
         src = PAD + width - 3 if side == 0 else PAD
         dst = PAD - 3 if side == 0 else PAD + width
-        start, stop = plan.spans[span]
-        slots = pl.ds(start, stop - start)
+        comp, comps, start, count = plan.sends[span]
+        comps, slots = pl.ds(comp, comps), pl.ds(start, count)
         return pltpu.make_async_remote_copy(
-            src_ref=xf.at[:, slots, pl.ds(src, 3), :],
-            dst_ref=xf.at[:, slots, pl.ds(dst, 3), :],
+            src_ref=xf.at[comps, slots, pl.ds(src, 3), :],
+            dst_ref=xf.at[comps, slots, pl.ds(dst, 3), :],
             send_sem=xs_sem.at[side, span],
             recv_sem=xr_sem.at[side, span],
             device_id=(right if side == 0 else left, d),
@@ -244,7 +248,7 @@
             device_id_type=MESH,
         )
 
-    spans = len(plan.spans)
+    spans = len(plan.sends)
 
     def along_y(level, carry):
         values = primitives(st, level)
@@ -306,7 +310,8 @@
     x_copy(0, 0).start()
     x_copy(1, 0).start()
     for span in range(1, spans):
-        lax.fori_loop(*plan.spans[span], along_x, 0)
+        if span == 1 and cells > most:
+            lax.fori_loop(most, cells, along_x, 0)
         x_copy(0, span).start()
         x_copy(1, span).start()
 
@@ -348,7 +353,7 @@
     lax.fori_loop(0, cells, depth_part, 0)
     ray_order(plan, levels, shifts, order)
 
-    x_row = {row: c for c, row in enumerate(ROWS[0])}
+    x_row = {row: c for c, row in enumerate(X_ROWS)}
 
     def advance(row, level, slot):
         value = part[row, level]
@@ -623,7 +628,7 @@
     state_shape = (8, cells, width, cross)
     lines_shape = (slabs, plan.packed, plan.rows, 128)
     fields_shape = (3, plan.positions, width, 128)
-    spans = len(plan.spans)
+    spans = len(plan.sends)
     state, fields = pl.pallas_call(
         functools.partial(section_kernel, plan),
         out_shape=(

time: 24.4 us -> 24.4 us (level)
  no operation moved by 1% of the time
where the time goes in v8:
time: 24.4 us; the launch traced here: 24.3 us
  Pallas kernels  23.6 us (97%)
  between operations  0.64 us (3%)
    pallas_call x1, Pallas kernels, per_device(): pl.pallas_call(functools.partial(section_kernel, plan), out_shape=(pltpu....  21.9 us
    pallas_call x1, Pallas kernels, per_device(): pl.pallas_call(functools.partial(ray_kernel, plan), out_shape=(jax.ShapeD...  1.78 us

profile of v8, /device:TPU:0, one launch (start us, length us, event | category | flops | bytes accessed | tf_op | source)
XLA Modules:
  0.0 24.3 jit_solution(13719098915629729104)
XLA Ops:
  0.6 21.9 %section.1 = (f32[8,16,16,128]{3,2,1,0:T(8,128)S(1)}, f32[3,24,16,128]{3,2,1,0:T(8,128)S(1)}) custom-call(s32[24]{0:T(128)} %levels_in.1, s32[24]{0:T(128)} %shifts_in.1, f32[16,16,128]{2,1,0:T(8,128)} %density.1, f32[3,16,16,128]{3,2,1,0:T(8,128)} %momentum.1, f32[3,16,16,128]{3,2,1,0:T(8,128)} %magnetic.1, f32[16,16,128]{2,1,0:T(8,128)} %energy.1), custom_call_target="tpu_custom_call" | custom-call | tf_op jit(solution)/shard_map/section/pallas_call | solution.py:632
  22.5 1.8 %ray.1 = (f32[8,16,16,128]{3,2,1,0:T(8,128)}, f32[512,48]{1,0:T(8,128)}) custom-call(f32[3,24,16,128]{3,2,1,0:T(8,128)S(1)} %get-tuple-element.6.fields, f32[8,16,16,128]{3,2,1,0:T(8,128)S(1)} %get-tuple-element.7.hold), custom_call_target="tpu_custom_call" | custom-call | tf_op jit(solution)/shard_map/ray/pallas_call | solution.py:675
